TPU v7x, 512 devices: a whole 4x4x16 slice. The times are simulated.
512 devices in a mesh: leaf: 128 (over y, z_lo, x, core), rank: 4 (over z_hi).
Axes of the slice: x: 4, y: 4, z: 16 (z_hi: 4, z_lo: 4; z = z_hi * 4 + z_lo), core: 2. Of those that a mesh axis runs over, the one named last changes fastest.
Arguments:
- load_vectors: bfloat16 [512, 4, 256], P('leaf'), may hold values from -6 to 6
- cluster_order: int32 [512, 256], P('leaf'), may hold values from 0 to 255, each once within a row
- block_present: int32 [8, 512], P(None, 'leaf'), may hold values 0 or 1
- factors: bfloat16 [8, 512, 2, 256, 256], P(None, 'leaf', None, 'rank'), may hold values from -0.25 to 0.25
Outputs:
- applied: float32 [512, 4, 256], P('leaf')
Inputs may be any that keep to these rules, and one draw needn't show every extreme that they name: `cluster_order`: each row is a permutation of 0 .. 255.
All inputs are finite; a program needn't handle non-finite values. No bound on the sum of `block_present` on one device may be relied on, other than what follows from the above.
Results may differ from a plain program's by a relative error of at most 0.012.
Values may be sent and summed in bfloat16 or wider, within the bound.
No kernel may reach another device: no remote copies, remote signals or barrier semaphores. Data moves between devices by JAX's collectives and lax.ppermute only.
A program may use at most 64 MiB of HBM per device.

v0:
```python
import jax
import jax.numpy as jnp
from jax import lax
from jax.sharding import PartitionSpec as P

LEVELS = 8


def swapped(block, axis, distance):
    count = lax.axis_size(axis)
    route = []
    for low in range(count):
        high = low | 1 << distance
        if high != low and high < count:
            route += [(low, high), (high, low)]
    return lax.ppermute(block, axis, route)


def total_of_pieces(shard, axis):
    return lax.all_gather(shard, axis).sum(0)


def partner_of(own_cols, level_bit, local_bits):
    if level_bit < local_bits:
        shaped = own_cols.reshape(
            (own_cols.shape[0] >> level_bit + 1, 2, 1 << level_bit) + own_cols.shape[1:]
        )
        return jnp.flip(shaped, 1).reshape(own_cols.shape)
    return swapped(own_cols, "leaf", level_bit - local_bits)


def level_terms(own_cols, weights, present, level_bit, local_bits):
    partner = partner_of(own_cols, level_bit, local_bits)
    own_term = jnp.einsum(
        "blc,bco->blo", own_cols, weights[:, 0], preferred_element_type=jnp.float32
    )
    off_term = jnp.einsum(
        "blc,bco->blo", partner, weights[:, 1], preferred_element_type=jnp.float32
    )
    return own_term + present.astype(jnp.float32)[:, None, None] * off_term


def local(load_vectors, cluster_order, block_present, factors):
    blocks = load_vectors.shape[0]
    local_bits = blocks.bit_length() - 1
    tree_bits = local_bits + lax.axis_size("leaf").bit_length() - 1
    columns = factors.shape[3]
    first_col = lax.axis_index("rank") * columns
    current = jnp.take_along_axis(load_vectors, cluster_order[:, None, :], axis=2).astype(
        jnp.float32
    )
    for level_idx in range(LEVELS):
        level_bit = (tree_bits - 1 - level_idx) % tree_bits
        rounded = current.astype(jnp.bfloat16)
        own_cols = lax.dynamic_slice_in_dim(rounded, first_col, columns, 2)
        terms = level_terms(
            own_cols, factors[level_idx], block_present[level_idx], level_bit, local_bits
        )
        current = total_of_pieces(terms, "rank")
    inverse = jnp.argsort(cluster_order, axis=1)
    return jnp.take_along_axis(current, inverse[:, None, :], axis=2)


def solution(mesh):
    in_specs = (
        P("leaf", None, None),
        P("leaf", None),
        P(None, "leaf"),
        P(None, "leaf", None, "rank", None),
    )
    out_specs = P("leaf", None, None)
    return jax.shard_map(local, mesh=mesh, in_specs=in_specs, out_specs=out_specs, check_vma=False)
```

profile of v0, /device:TPU:28, one launch (start us, length us, event | category | flops | bytes accessed | tf_op | source)
XLA Modules:
  0.0 223.3 jit_solution(17575114213110370803)
XLA Ops:
  6.5 0.6 iota.7
  7.1 0.1 sort.19.cloned.1.call-update
  7.3 0.0 copy-start
  7.3 0.0 copy-start.2
  7.3 1.6 fusion.20
  8.9 0.3 convert_reduce_fusion
  9.3 0.2 copy.26
  9.5 0.0 copy-start.1
  9.7 2.8 %sort.19.cloned.1.call-done = (s32[4,256]{1,0:T(4,128)}, s32[4,256]{1,0:T(4,128)}) async-done(((s32[4,256]{1,0:T(4,128)}, s32[4,256]{1,0:T(4,128)}), (s32[4,256]{1,0:T(4,128)}, s32[4,256]{1,0:T(4,128)})) %sort.19.cloned.1.call-update) | async-done | bytes 8208 | tf_op jit(solution)/shard_map/jit(argsort)/sort | solution.py:60
  12.5 0.7 compare_and_fusion
  13.2 0.7 fusion.16
  13.9 5.8 %gather_fusion = bf16[1024,4]{1,0:T(8,128)(2,1)S(1)} fusion(bf16[4,4,256]{1,2,0:T(8,128)(2,1)S(1)} %copy.26, s32[1024]{0:T(1024)S(1)} %bitcast.119), kind=kCustom, calls=%fused_computation | custom fusion | bytes 24576 | tf_op jit(solution)/shard_map/jit(take_along_axis)/gather | solution.py:49
  19.7 0.1 copy.27
  19.9 0.1 constant_dynamic-slice_fusion
  19.9 0.1 fusion.18
  20.0 3.1 %collective-permute-start = (bf16[4,4,64]{2,1,0:T(4,128)(2,1)S(1)}, bf16[4,4,64]{2,1,0:T(4,128)(2,1)S(1)}, u32[]{:S(2)}, u32[]{:S(2)}) collective-permute-start(bf16[4,4,64]{2,1,0:T(4,128)(2,1)S(1)} %fusion.18), channel_id=1, source_target_pairs={{0,256},{256,0},{4,260},{260,4},{8,264},{264,8},{12,268},{268,12},... | collective-permute-start | bytes 6152 | tf_op jit(solution)/shard_map/ppermute | solution.py:16
  23.2 0.2 fusion.15
  23.4 3.7 %collective-permute-done = bf16[4,4,64]{2,1,0:T(4,128)(2,1)S(1)} collective-permute-done((bf16[4,4,64]{2,1,0:T(4,128)(2,1)S(1)}, bf16[4,4,64]{2,1,0:T(4,128)(2,1)S(1)}, u32[]{:S(2)}, u32[]{:S(2)}) %collective-permute-start) | collective-permute-done | bytes 2080 | tf_op jit(solution)/shard_map/ppermute | solution.py:16
  27.0 0.1 fusion.7
  27.1 25.7 %all-gather = f32[16,4,256]{2,1,0:T(4,128)S(1)} all-gather(f32[4,4,256]{2,1,0:T(4,128)S(1)} %fusion.7), channel_id=2, replica_groups=mesh['leaf'=128,'rank'=4] {'rank'}, dimensions={0}, use_global_device_ids=true | all-gather | bytes 81920 | tf_op jit(solution)/shard_map/all_gather | solution.py:20
  52.9 0.1 dynamic-slice_convert_fusion.6
  53.0 2.6 %collective-permute-start.1 = (bf16[4,4,64]{2,1,0:T(4,128)(2,1)S(1)}, bf16[4,4,64]{2,1,0:T(4,128)(2,1)S(1)}, u32[]{:S(2)}, u32[]{:S(2)}) collective-permute-start(bf16[4,4,64]{2,1,0:T(4,128)(2,1)S(1)} %dynamic-slice_convert_fusion.6), channel_id=1, source_target_pairs={{0,128},{128,0},{4,132},{132,4},{8,136},{136,8},{12,140},{140,12},... | collective-permute-start | bytes 6152 | tf_op jit(solution)/shard_map/ppermute | solution.py:16
  55.6 0.1 fusion.14
  55.8 2.7 %collective-permute-done.1 = bf16[4,4,64]{2,1,0:T(4,128)(2,1)S(1)} collective-permute-done((bf16[4,4,64]{2,1,0:T(4,128)(2,1)S(1)}, bf16[4,4,64]{2,1,0:T(4,128)(2,1)S(1)}, u32[]{:S(2)}, u32[]{:S(2)}) %collective-permute-start.1) | collective-permute-done | bytes 2080 | tf_op jit(solution)/shard_map/ppermute | solution.py:16
  58.5 0.1 fusion.6
  58.6 17.3 %all-gather.1 = f32[16,4,256]{2,1,0:T(4,128)S(1)} all-gather(f32[4,4,256]{2,1,0:T(4,128)S(1)} %fusion.6), channel_id=3, replica_groups=mesh['leaf'=128,'rank'=4] {'rank'}, dimensions={0}, use_global_device_ids=true | all-gather | bytes 81920 | tf_op jit(solution)/shard_map/all_gather | solution.py:20
  75.9 0.1 dynamic-slice_convert_fusion.5
  76.0 3.4 %collective-permute-start.2 = (bf16[4,4,64]{2,1,0:T(4,128)(2,1)S(1)}, bf16[4,4,64]{2,1,0:T(4,128)(2,1)S(1)}, u32[]{:S(2)}, u32[]{:S(2)}) collective-permute-start(bf16[4,4,64]{2,1,0:T(4,128)(2,1)S(1)} %dynamic-slice_convert_fusion.5), channel_id=1, source_target_pairs={{0,64},{64,0},{4,68},{68,4},{8,72},{72,8},{12,76},{76,12},{16,80},... | collective-permute-start | bytes 6152 | tf_op jit(solution)/shard_map/ppermute | solution.py:16
  79.3 0.1 fusion.13
  79.5 2.9 %collective-permute-done.2 = bf16[4,4,64]{2,1,0:T(4,128)(2,1)S(1)} collective-permute-done((bf16[4,4,64]{2,1,0:T(4,128)(2,1)S(1)}, bf16[4,4,64]{2,1,0:T(4,128)(2,1)S(1)}, u32[]{:S(2)}, u32[]{:S(2)}) %collective-permute-start.2) | collective-permute-done | bytes 2080 | tf_op jit(solution)/shard_map/ppermute | solution.py:16
  82.3 0.1 fusion.5
  82.4 17.3 %all-gather.2 = f32[16,4,256]{2,1,0:T(4,128)S(1)} all-gather(f32[4,4,256]{2,1,0:T(4,128)S(1)} %fusion.5), channel_id=4, replica_groups=mesh['leaf'=128,'rank'=4] {'rank'}, dimensions={0}, use_global_device_ids=true | all-gather | bytes 81920 | tf_op jit(solution)/shard_map/all_gather | solution.py:20
  99.8 0.1 dynamic-slice_convert_fusion.4
  99.8 3.0 %collective-permute-start.3 = (bf16[4,4,64]{2,1,0:T(4,128)(2,1)S(1)}, bf16[4,4,64]{2,1,0:T(4,128)(2,1)S(1)}, u32[]{:S(2)}, u32[]{:S(2)}) collective-permute-start(bf16[4,4,64]{2,1,0:T(4,128)(2,1)S(1)} %dynamic-slice_convert_fusion.4), channel_id=1, source_target_pairs={{0,32},{32,0},{4,36},{36,4},{8,40},{40,8},{12,44},{44,12},{16,48},... | collective-permute-start | bytes 6152 | tf_op jit(solution)/shard_map/ppermute | solution.py:16
  102.8 0.1 fusion.12
  103.0 2.4 %collective-permute-done.3 = bf16[4,4,64]{2,1,0:T(4,128)(2,1)S(1)} collective-permute-done((bf16[4,4,64]{2,1,0:T(4,128)(2,1)S(1)}, bf16[4,4,64]{2,1,0:T(4,128)(2,1)S(1)}, u32[]{:S(2)}, u32[]{:S(2)}) %collective-permute-start.3) | collective-permute-done | bytes 2080 | tf_op jit(solution)/shard_map/ppermute | solution.py:16
  105.3 0.1 fusion.4
  105.4 17.3 %all-gather.3 = f32[16,4,256]{2,1,0:T(4,128)S(1)} all-gather(f32[4,4,256]{2,1,0:T(4,128)S(1)} %fusion.4), channel_id=5, replica_groups=mesh['leaf'=128,'rank'=4] {'rank'}, dimensions={0}, use_global_device_ids=true | all-gather | bytes 81920 | tf_op jit(solution)/shard_map/all_gather | solution.py:20
  122.8 0.1 dynamic-slice_convert_fusion.3
  122.9 2.4 %collective-permute-start.4 = (bf16[4,4,64]{2,1,0:T(4,128)(2,1)S(1)}, bf16[4,4,64]{2,1,0:T(4,128)(2,1)S(1)}, u32[]{:S(2)}, u32[]{:S(2)}) collective-permute-start(bf16[4,4,64]{2,1,0:T(4,128)(2,1)S(1)} %dynamic-slice_convert_fusion.3), channel_id=1, source_target_pairs={{0,16},{16,0},{4,20},{20,4},{8,24},{24,8},{12,28},{28,12},{32,48},... | collective-permute-start | bytes 6152 | tf_op jit(solution)/shard_map/ppermute | solution.py:16
  125.2 0.1 fusion.11
  125.4 4.5 %collective-permute-done.4 = bf16[4,4,64]{2,1,0:T(4,128)(2,1)S(1)} collective-permute-done((bf16[4,4,64]{2,1,0:T(4,128)(2,1)S(1)}, bf16[4,4,64]{2,1,0:T(4,128)(2,1)S(1)}, u32[]{:S(2)}, u32[]{:S(2)}) %collective-permute-start.4) | collective-permute-done | bytes 2080 | tf_op jit(solution)/shard_map/ppermute | solution.py:16
  129.9 0.1 fusion.3
  130.0 17.4 %all-gather.4 = f32[16,4,256]{2,1,0:T(4,128)S(1)} all-gather(f32[4,4,256]{2,1,0:T(4,128)S(1)} %fusion.3), channel_id=6, replica_groups=mesh['leaf'=128,'rank'=4] {'rank'}, dimensions={0}, use_global_device_ids=true | all-gather | bytes 81920 | tf_op jit(solution)/shard_map/all_gather | solution.py:20
  147.4 0.1 dynamic-slice_convert_fusion.2
  147.4 3.1 %collective-permute-start.5 = (bf16[4,4,64]{2,1,0:T(4,128)(2,1)S(1)}, bf16[4,4,64]{2,1,0:T(4,128)(2,1)S(1)}, u32[]{:S(2)}, u32[]{:S(2)}) collective-permute-start(bf16[4,4,64]{2,1,0:T(4,128)(2,1)S(1)} %dynamic-slice_convert_fusion.2), channel_id=1, source_target_pairs={{0,8},{8,0},{4,12},{12,4},{16,24},{24,16},{20,28},{28,20},{32,40},... | collective-permute-start | bytes 6152 | tf_op jit(solution)/shard_map/ppermute | solution.py:16
  150.5 0.1 fusion.10
  150.6 2.3 %collective-permute-done.5 = bf16[4,4,64]{2,1,0:T(4,128)(2,1)S(1)} collective-permute-done((bf16[4,4,64]{2,1,0:T(4,128)(2,1)S(1)}, bf16[4,4,64]{2,1,0:T(4,128)(2,1)S(1)}, u32[]{:S(2)}, u32[]{:S(2)}) %collective-permute-start.5) | collective-permute-done | bytes 2080 | tf_op jit(solution)/shard_map/ppermute | solution.py:16
  152.9 0.1 fusion.2
  153.0 17.3 %all-gather.5 = f32[16,4,256]{2,1,0:T(4,128)S(1)} all-gather(f32[4,4,256]{2,1,0:T(4,128)S(1)} %fusion.2), channel_id=7, replica_groups=mesh['leaf'=128,'rank'=4] {'rank'}, dimensions={0}, use_global_device_ids=true | all-gather | bytes 81920 | tf_op jit(solution)/shard_map/all_gather | solution.py:20
  170.3 0.1 dynamic-slice_convert_fusion.1
  170.4 1.9 collective-permute-start.6
  172.3 0.1 fusion.9
  172.5 1.0 collective-permute-done.6
  173.5 0.1 fusion.1
  173.6 17.4 %all-gather.6 = f32[16,4,256]{2,1,0:T(4,128)S(1)} all-gather(f32[4,4,256]{2,1,0:T(4,128)S(1)} %fusion.1), channel_id=8, replica_groups=mesh['leaf'=128,'rank'=4] {'rank'}, dimensions={0}, use_global_device_ids=true | all-gather | bytes 81920 | tf_op jit(solution)/shard_map/all_gather | solution.py:20
  191.0 0.1 dynamic-slice_convert_fusion
  191.1 0.1 fusion.8
  191.2 0.1 fusion
  191.3 17.3 %all-gather.7 = f32[16,4,256]{2,1,0:T(4,128)S(1)} all-gather(f32[4,4,256]{2,1,0:T(4,128)S(1)} %fusion), channel_id=9, replica_groups=mesh['leaf'=128,'rank'=4] {'rank'}, dimensions={0}, use_global_device_ids=true | all-gather | bytes 81920 | tf_op jit(solution)/shard_map/all_gather | solution.py:20
  208.6 0.2 copy.36
  208.8 6.8 %gather_fusion.1 = f32[1024,4]{1,0:T(8,128)S(1)} fusion(f32[4,4,256]{1,2,0:T(8,128)S(1)} %copy.36, s32[1024]{0:T(1024)S(1)} %bitcast.120), kind=kCustom, calls=%fused_computation.1 | custom fusion | bytes 40960 | tf_op jit(solution)/shard_map/jit(take_along_axis)/gather | solution.py:61
  215.6 0.2 copy.37
  215.8 0.6 select_bitcast_fusion
  (23 shorter events, 0.3 us)
Async XLA Ops:
  6.5 6.0 %sort.19.cloned.1.call-start = ((), (), s32[]{:S(2)}) async-start(), calls=%async_computation | async-start | bytes 24608 | tf_op jit(solution)/shard_map/jit(argsort)/sort | solution.py:60
  7.3 1.7 copy-start
  7.3 2.0 copy-start.2
  9.5 3.1 %copy-start.1 = (s32[4,256]{1,0:T(4,128)S(1)}, s32[4,256]{1,0:T(4,128)}, u32[]{:S(2)}) copy-start(s32[4,256]{1,0:T(4,128)} %param.5) | copy-start | bytes 12292
  20.0 7.0 %collective-permute-start = (bf16[4,4,64]{2,1,0:T(4,128)(2,1)S(1)}, bf16[4,4,64]{2,1,0:T(4,128)(2,1)S(1)}, u32[]{:S(2)}, u32[]{:S(2)}) collective-permute-start(bf16[4,4,64]{2,1,0:T(4,128)(2,1)S(1)} %fusion.18), channel_id=1, source_target_pairs={{0,256},{256,0},{4,260},{260,4},{8,264},{264,8},{12,268},{268,12},... | collective-permute-start | bytes 6152 | tf_op jit(solution)/shard_map/ppermute | solution.py:16
  53.0 5.5 %collective-permute-start.1 = (bf16[4,4,64]{2,1,0:T(4,128)(2,1)S(1)}, bf16[4,4,64]{2,1,0:T(4,128)(2,1)S(1)}, u32[]{:S(2)}, u32[]{:S(2)}) collective-permute-start(bf16[4,4,64]{2,1,0:T(4,128)(2,1)S(1)} %dynamic-slice_convert_fusion.6), channel_id=1, source_target_pairs={{0,128},{128,0},{4,132},{132,4},{8,136},{136,8},{12,140},{140,12},... | collective-permute-start | bytes 6152 | tf_op jit(solution)/shard_map/ppermute | solution.py:16
  76.0 6.4 %collective-permute-start.2 = (bf16[4,4,64]{2,1,0:T(4,128)(2,1)S(1)}, bf16[4,4,64]{2,1,0:T(4,128)(2,1)S(1)}, u32[]{:S(2)}, u32[]{:S(2)}) collective-permute-start(bf16[4,4,64]{2,1,0:T(4,128)(2,1)S(1)} %dynamic-slice_convert_fusion.5), channel_id=1, source_target_pairs={{0,64},{64,0},{4,68},{68,4},{8,72},{72,8},{12,76},{76,12},{16,80},... | collective-permute-start | bytes 6152 | tf_op jit(solution)/shard_map/ppermute | solution.py:16
  99.8 5.5 %collective-permute-start.3 = (bf16[4,4,64]{2,1,0:T(4,128)(2,1)S(1)}, bf16[4,4,64]{2,1,0:T(4,128)(2,1)S(1)}, u32[]{:S(2)}, u32[]{:S(2)}) collective-permute-start(bf16[4,4,64]{2,1,0:T(4,128)(2,1)S(1)} %dynamic-slice_convert_fusion.4), channel_id=1, source_target_pairs={{0,32},{32,0},{4,36},{36,4},{8,40},{40,8},{12,44},{44,12},{16,48},... | collective-permute-start | bytes 6152 | tf_op jit(solution)/shard_map/ppermute | solution.py:16
  122.9 7.0 %collective-permute-start.4 = (bf16[4,4,64]{2,1,0:T(4,128)(2,1)S(1)}, bf16[4,4,64]{2,1,0:T(4,128)(2,1)S(1)}, u32[]{:S(2)}, u32[]{:S(2)}) collective-permute-start(bf16[4,4,64]{2,1,0:T(4,128)(2,1)S(1)} %dynamic-slice_convert_fusion.3), channel_id=1, source_target_pairs={{0,16},{16,0},{4,20},{20,4},{8,24},{24,8},{12,28},{28,12},{32,48},... | collective-permute-start | bytes 6152 | tf_op jit(solution)/shard_map/ppermute | solution.py:16
  147.4 5.5 %collective-permute-start.5 = (bf16[4,4,64]{2,1,0:T(4,128)(2,1)S(1)}, bf16[4,4,64]{2,1,0:T(4,128)(2,1)S(1)}, u32[]{:S(2)}, u32[]{:S(2)}) collective-permute-start(bf16[4,4,64]{2,1,0:T(4,128)(2,1)S(1)} %dynamic-slice_convert_fusion.2), channel_id=1, source_target_pairs={{0,8},{8,0},{4,12},{12,4},{16,24},{24,16},{20,28},{28,20},{32,40},... | collective-permute-start | bytes 6152 | tf_op jit(solution)/shard_map/ppermute | solution.py:16
  170.4 3.1 %collective-permute-start.6 = (bf16[4,4,64]{2,1,0:T(4,128)(2,1)S(1)}, bf16[4,4,64]{2,1,0:T(4,128)(2,1)S(1)}, u32[]{:S(2)}, u32[]{:S(2)}) collective-permute-start(bf16[4,4,64]{2,1,0:T(4,128)(2,1)S(1)} %dynamic-slice_convert_fusion.1), channel_id=1, source_target_pairs={{0,4},{4,0},{8,12},{12,8},{16,20},{20,16},{24,28},{28,24},{32,36},... | collective-permute-start | bytes 6152 | tf_op jit(solution)/shard_map/ppermute | solution.py:16
Sparse Core Ops, SparseCore 0:
  9.7 2.5 sort.21.cloned.1.call-done
  (1 shorter events, 0.0 us)
where the time goes:
time: 224 us; the launch traced here: 223 us
  blocking collectives  147 us (66%)
  starting transfers between devices  19.5 us (9%)
  local copies, waits for them, and re-layouts  19.4 us (9%)
  waiting for transfers between devices  19.4 us (9%)
  between operations  13.6 us (6%)
  other arithmetic  2.54 us (1%)
    all_gather x8, blocking collectives, total_of_pieces(): return lax.all_gather(shard, axis).sum(0)  147 us
    ppermute x7, starting transfers between devices, swapped(): return lax.ppermute(block, axis, route)  19.5 us
    ppermute x7, waiting for transfers between devices, swapped(): return lax.ppermute(block, axis, route)  19.4 us
    gather x2, local copies, waits for them, and re-layouts, local(): return jnp.take_along_axis(current, inverse[:, None, :], axis=2)  6.98 us
    gather x2, local copies, waits for them, and re-layouts, local(): jnp.take_along_axis(load_vectors, cluster_order[:, None, :], axis=2)  5.96 us
  transfers between devices with their start and end apart: 7, of which 7 were waited for; matrix products, arithmetic and copies ran while one was open for 0% of the time, Pallas kernels for 0%

commit v1 on v0

v1 whole, which is shorter than its diff:
```python
import jax
import jax.numpy as jnp
from jax import lax
from jax.sharding import PartitionSpec as P

LEVELS = 8
F32 = jnp.float32
BF16 = jnp.bfloat16


def left_half():
    return lax.broadcasted_iota(jnp.int32, (8, 128), 1) < 64


def turned(tile):
    return jnp.concatenate([tile[:, 64:], tile[:, :64]], axis=1)


def own_columns(loads, order, rank):
    quarter = lax.dynamic_slice_in_dim(order, 64 * rank, 64, 1)
    pick = (jnp.arange(256)[None, :, None] == quarter[:, None, :]).astype(BF16)
    got = jnp.einsum("blc,bco->blo", loads, pick, preferred_element_type=F32)
    return jnp.concatenate([got[:2].reshape(8, 64), got[2:].reshape(8, 64)], axis=1)


def product(own, partner, mask, weights):
    left = left_half()
    top = jnp.where(left, own, turned(partner))
    bottom = jnp.where(left, turned(own), partner)
    cols = jnp.concatenate([top, bottom], axis=0).astype(BF16)
    wide = jnp.concatenate([cols] * 4, axis=1) * mask
    return jnp.dot(wide, weights, preferred_element_type=F32)


def chunks(part, copies):
    left = left_half()
    pieces = []
    for at in range(2):
        tile = part[:, 128 * at : 128 * (at + 1)]
        top, bottom = tile[:8], tile[8:]
        pieces += [jnp.where(left, top, turned(bottom)), jnp.where(left, turned(top), bottom)]
    return jnp.broadcast_to(jnp.stack(pieces)[None], (copies, 4, 8, 128)).reshape(copies * 4, 8, 128)


def put_back(state, order):
    high = state.astype(BF16)
    rest = state - high.astype(F32)
    middle = rest.astype(BF16)
    low = (rest - middle.astype(F32)).astype(BF16)
    pieces = jnp.concatenate([high, middle, low], axis=0).reshape(3, 4, 4, 256)
    pick = (jnp.arange(256)[None, :, None] == order[:, None, :]).astype(BF16)
    put = jnp.einsum("pblj,bij->pbli", pieces, pick, preferred_element_type=F32)
    return put[0] + put[1] + put[2]


def pair_groups(leaves, ranks, bit):
    groups = []
    for leaf in range(leaves):
        if not leaf >> bit & 1:
            groups.append([at * ranks + r for at in (leaf, leaf | 1 << bit) for r in range(ranks)])
    return groups


def masks(present):
    block_of = jnp.arange(16) // 4
    wide = jnp.arange(512)
    same = block_of[:, None] == (wide // 128)[None, :]
    own = (wide % 128 < 64)[None, None, :]
    there = jnp.repeat(present, 4, axis=1)[:, :, None] != 0
    return jnp.where(same[None] & (own | there), 1.0, 0.0).astype(BF16)


def local(load_vectors, cluster_order, block_present, factors):
    leaves, ranks = lax.axis_size("leaf"), lax.axis_size("rank")
    leaf_bits = leaves.bit_length() - 1
    leaf, rank = lax.axis_index("leaf"), lax.axis_index("rank")
    weights = factors.reshape(LEVELS, 512, 256)
    mask = masks(block_present)
    own = own_columns(load_vectors, cluster_order, rank)
    partner = lax.ppermute(own, "leaf", [(at, at ^ 1 << leaf_bits - 1) for at in range(leaves)])
    uppers = [(leaf >> bit & 1) != 0 for bit in range(leaf_bits - 1)]
    partner, *uppers = lax.optimization_barrier((partner, *uppers))
    for level in range(LEVELS):
        part = product(own, partner, mask[level], weights[level])
        bit = leaf_bits - 2 - level
        if bit >= 0:
            received = lax.all_to_all(
                chunks(part, 2), ("leaf", "rank"), 0, 0, axis_index_groups=pair_groups(leaves, ranks, bit), tiled=True
            )
            upper = uppers[bit]
            low, high = received[:4].sum(0), received[4:].sum(0)
            own = jnp.where(upper, high, low)
            partner = jnp.where(upper, low, high)
        elif level < LEVELS - 1:
            own = lax.all_to_all(chunks(part, 1), "rank", 0, 0, tiled=True).sum(0)
            partner = turned(own)
    whole = lax.all_to_all(jnp.stack([part] * ranks), "rank", 0, 0, tiled=True).sum(0)
    return put_back(whole, cluster_order)


def solution(mesh):
    in_specs = (
        P("leaf", None, None),
        P("leaf", None),
        P(None, "leaf"),
        P(None, "leaf", None, "rank", None),
    )
    out_specs = P("leaf", None, None)
    return jax.shard_map(local, mesh=mesh, in_specs=in_specs, out_specs=out_specs, check_vma=False)
```

time: 224 us -> 155 us (0.69)
  the two profiles are of different devices: /device:TPU:28 before, /device:TPU:16 now
where the time goes in v1:
time: 155 us; the launch traced here: 154 us
  blocking collectives  137 us (88%)
  starting transfers between devices  7.59 us (5%)
  local copies, waits for them, and re-layouts  4.14 us (3%)
  other arithmetic  3.39 us (2%)
  matrix products  1.67 us (1%)
    all_to_all x6, blocking collectives, local(): lax.all_to_all(chunks(part, 2), ('leaf', 'rank'), 0, 0, axis_index_groups...  106 us
    all_to_all x1, blocking collectives, local(): lax.all_to_all(jnp.stack([part] * ranks), 'rank', 0, 0, tiled=True).sum(0)  16 us
    all_to_all x1, blocking collectives, local(): own = lax.all_to_all(chunks(part, 1), 'rank', 0, 0, tiled=True).sum(0)  15 us
    ppermute x1, starting transfers between devices, local(): lax.ppermute(own, 'leaf', [(at, at ^ 1 << leaf_bits - 1) for at in range(...  7.59 us
  transfers between devices with their start and end apart: 1, of which 0 were waited for; matrix products, arithmetic and copies ran while one was open for 2% of the time, Pallas kernels for 0%

profile of v1, /device:TPU:16, one launch (start us, length us, event | category | flops | bytes accessed | tf_op | source)
XLA Modules:
  0.0 154.1 jit_solution(14057783246268777045)
XLA Ops:
  0.0 0.8 constant_dynamic-slice_fusion
  0.8 0.2 convolution_bitcast_fusion.1
  1.0 0.1 pad_maximum_fusion.8
  1.1 7.6 %collective-permute-start = (bf16[8,128]{1,0:T(8,128)(2,1)S(1)}, bf16[8,128]{1,0:T(8,128)(2,1)S(1)}, u32[]{:S(2)}, u32[]{:S(2)}) collective-permute-start(bf16[8,128]{1,0:T(8,128)(2,1)S(1)} %pad_maximum_fusion.8), channel_id=1, source_target_pairs={{0,256},{4,260},{8,264},{12,268},{16,272},{20,276},{24,280},{28,28... | collective-permute-start | bytes 6152 | tf_op jit(solution)/shard_map/ppermute | solution.py:80
  8.7 0.7 broadcast_compare_fusion.1
  9.4 0.1 copy.8
  9.5 1.6 %fusion.223 = (bf16[1,4,2,64,256]{4,3,2,1,0:T(8,128)(2,1)S(1)}, bf16[1,4,2,64,256]{4,3,2,1,0:T(8,128)(2,1)S(1)}, bf16[1,4,2,64,256]{4,3,2,1,0:T(8,128)(2,1)S(1)}...) fusion(bf16[8,4,2,64,256]{4,3,2,1,0:T(8,128)(2,1)} %param.7), kind=kLoop, calls=%fused_computation.319 | loop fusion | bytes 4194304 | tf_op jit(solution)/shard_map/slice | solution.py:84
  11.1 0.1 broadcast_compare_fusion
  11.2 0.1 select_convert_fusion
  11.4 0.1 fusion.246
  11.5 0.1 fusion.212
  11.5 0.1 fusion.28
  11.7 0.1 fusion.231
  11.8 0.1 fusion.178
  11.8 25.8 %all_to_all.40 = f32[8,8,128]{2,1,0:T(8,128)S(1)} all-to-all(f32[8,8,128]{2,1,0:T(8,128)S(1)} %bitcast.156), channel_id=1, replica_groups={{0,1,2,3,128,129,130,131},{4,5,6,7,132,133,134,135},{8,9,10,11,136,137,..., dimensions={0} | all-to-all | bytes 65536 | tf_op jit(solution)/shard_map/all_to_all | solution.py:87
  37.6 0.1 fusion.245
  37.7 0.1 fusion.210
  37.9 0.1 fusion.209
  37.9 0.1 fusion.25
  38.1 0.1 fusion.230
  38.2 0.1 fusion.174
  38.3 15.1 %all_to_all.41 = f32[8,8,128]{2,1,0:T(8,128)S(1)} all-to-all(f32[8,8,128]{2,1,0:T(8,128)S(1)} %bitcast.157), channel_id=1, replica_groups={{0,1,2,3,64,65,66,67},{4,5,6,7,68,69,70,71},{8,9,10,11,72,73,74,75},{12..., dimensions={0} | all-to-all | bytes 65536 | tf_op jit(solution)/shard_map/all_to_all | solution.py:87
  53.4 0.1 fusion.243
  53.5 0.1 fusion.208
  53.6 0.1 fusion.242
  53.6 0.1 fusion.207
  53.7 0.1 fusion.22
  53.9 0.1 fusion.229
  53.9 0.1 fusion.170
  54.0 15.1 %all_to_all.42 = f32[8,8,128]{2,1,0:T(8,128)S(1)} all-to-all(f32[8,8,128]{2,1,0:T(8,128)S(1)} %bitcast.158), channel_id=1, replica_groups={{0,1,2,3,32,33,34,35},{4,5,6,7,36,37,38,39},{8,9,10,11,40,41,42,43},{12..., dimensions={0} | all-to-all | bytes 65536 | tf_op jit(solution)/shard_map/all_to_all | solution.py:87
  69.2 0.1 fusion.241
  69.2 0.1 fusion.206
  69.4 0.1 fusion.205
  69.5 0.1 fusion.19
  69.6 0.1 fusion.228
  69.7 0.1 fusion.166
  69.8 19.4 %all_to_all.43 = f32[8,8,128]{2,1,0:T(8,128)S(1)} all-to-all(f32[8,8,128]{2,1,0:T(8,128)S(1)} %bitcast.159), channel_id=1, replica_groups={{0,1,2,3,16,17,18,19},{4,5,6,7,20,21,22,23},{8,9,10,11,24,25,26,27},{12..., dimensions={0} | all-to-all | bytes 65536 | tf_op jit(solution)/shard_map/all_to_all | solution.py:87
  89.2 0.1 fusion.239
  89.2 0.1 fusion.204
  89.4 0.1 fusion.203
  89.5 0.1 fusion.16
  89.6 0.1 fusion.227
  89.7 0.1 fusion.162
  89.8 15.9 %all_to_all.44 = f32[8,8,128]{2,1,0:T(8,128)S(1)} all-to-all(f32[8,8,128]{2,1,0:T(8,128)S(1)} %bitcast.160), channel_id=1, replica_groups={{0,1,2,3,8,9,10,11},{4,5,6,7,12,13,14,15},{16,17,18,19,24,25,26,27},{20..., dimensions={0} | all-to-all | bytes 65536 | tf_op jit(solution)/shard_map/all_to_all | solution.py:87
  105.7 0.1 fusion.237
  105.7 0.1 fusion.202
  105.9 0.1 fusion.201
  106.0 0.1 fusion.13
  106.1 0.1 fusion.226
  106.2 0.1 fusion.158
  106.3 15.0 %all_to_all.45 = f32[8,8,128]{2,1,0:T(8,128)S(1)} all-to-all(f32[8,8,128]{2,1,0:T(8,128)S(1)} %bitcast.161), channel_id=1, replica_groups={{0,1,2,3,4,5,6,7},{8,9,10,11,12,13,14,15},{16,17,18,19,20,21,22,23},{24..., dimensions={0} | all-to-all | bytes 65536 | tf_op jit(solution)/shard_map/all_to_all | solution.py:87
  121.3 0.1 fusion.235
  121.4 0.1 fusion.200
  121.5 0.1 fusion.199
  121.6 0.1 fusion.10
  121.8 0.1 fusion.225
  121.8 0.1 fusion.154
  121.9 15.0 %all_to_all.46 = f32[4,8,128]{2,1,0:T(8,128)S(1)} all-to-all(f32[4,8,128]{2,1,0:T(8,128)S(1)} %pad_maximum_fusion.7), channel_id=1, replica_groups=mesh['leaf'=128,'rank'=4] {'rank'}, dimensions={0} | all-to-all | bytes 32768 | tf_op jit(solution)/shard_map/all_to_all | solution.py:95
  136.9 0.1 fusion.233
  137.0 0.1 maximum_bitcast_fusion
  137.0 0.1 fusion.7
  137.2 16.0 %all_to_all.47 = f32[4,16,256]{2,1,0:T(8,128)S(1)} all-to-all(f32[4,16,256]{2,1,0:T(8,128)S(1)} %stack.147), channel_id=1, replica_groups=mesh['leaf'=128,'rank'=4] {'rank'}, dimensions={0} | all-to-all | bytes 131072 | tf_op jit(solution)/shard_map/all_to_all | solution.py:97
  153.2 0.3 convolution_bitcast_fusion
  153.5 0.6 fusion.5
  (47 shorter events, 0.6 us)
Async XLA Ops:
  0.0 0.8 copy-start
  1.1 10.3 %collective-permute-start = (bf16[8,128]{1,0:T(8,128)(2,1)S(1)}, bf16[8,128]{1,0:T(8,128)(2,1)S(1)}, u32[]{:S(2)}, u32[]{:S(2)}) collective-permute-start(bf16[8,128]{1,0:T(8,128)(2,1)S(1)} %pad_maximum_fusion.8), channel_id=1, source_target_pairs={{0,256},{4,260},{8,264},{12,268},{16,272},{20,276},{24,280},{28,28... | collective-permute-start | bytes 6152 | tf_op jit(solution)/shard_map/ppermute | solution.py:80
  53.4 99.8 %copy-start.1 = (s32[4,256]{1,0:T(4,128)S(1)}, s32[4,256]{1,0:T(4,128)}, u32[]{:S(2)}) copy-start(s32[4,256]{1,0:T(4,128)} %param.5) | copy-start | bytes 12292

commit v2 on v1

--- a/solution.py
+++ b/solution.py
@@ -6,6 +6,8 @@
 LEVELS = 8
 F32 = jnp.float32
 BF16 = jnp.bfloat16
+WIDE = BF16
+BY_COLUMNS = (4, 6)
 
 
 def left_half():
@@ -70,31 +72,108 @@
     return jnp.where(same[None] & (own | there), 1.0, 0.0).astype(BF16)
 
 
+def piece_for(pieces, quarter):
+    return lax.dynamic_index_in_dim(pieces, quarter, 0, keepdims=False)
+
+
+def column_pieces(weights):
+    parts = [jnp.concatenate([weights[:, 0, :, 64 * q : 64 * q + 64], weights[:, 1, :, 64 * q : 64 * q + 64]], 2) for q in range(4)]
+    return jnp.stack(parts)
+
+
+def assembled(*pieces):
+    return jnp.stack([pieces[0], pieces[3], pieces[2], pieces[1]], axis=1).reshape(1024, 128)
+
+
+def column_product(own, partner, mask, columns, rank):
+    both = jnp.concatenate([own, partner], axis=0).astype(BF16)
+    turn = lax.dynamic_slice_in_dim(jnp.concatenate([both, both], axis=1), 64 * rank, 256, 1)
+    got = jnp.dot(jnp.concatenate([turn] * 4, axis=1) * mask, columns, preferred_element_type=F32)
+    got = got[:16, :64] + got[16:, 64:]
+    return jnp.concatenate([got[:8], got[8:]], axis=1)
+
+
+def column_masks(present):
+    block_of = jnp.arange(16) // 4
+    same = block_of[:, None] == (jnp.arange(1024) // 256)[None, :]
+    there = jnp.repeat(present, 4)[:, None] != 0
+    return jnp.where(jnp.concatenate([same, same & there], axis=0), 1.0, 0.0).astype(BF16)
+
+
+def by_side(received, upper):
+    low, high = received[:4].astype(F32).sum(0), received[4:].astype(F32).sum(0)
+    return jnp.where(upper, high, low), jnp.where(upper, low, high)
+
+
 def local(load_vectors, cluster_order, block_present, factors):
     leaves, ranks = lax.axis_size("leaf"), lax.axis_size("rank")
     leaf_bits = leaves.bit_length() - 1
     leaf, rank = lax.axis_index("leaf"), lax.axis_index("rank")
-    weights = factors.reshape(LEVELS, 512, 256)
-    mask = masks(block_present)
     own = own_columns(load_vectors, cluster_order, rank)
     partner = lax.ppermute(own, "leaf", [(at, at ^ 1 << leaf_bits - 1) for at in range(leaves)])
     uppers = [(leaf >> bit & 1) != 0 for bit in range(leaf_bits - 1)]
-    partner, *uppers = lax.optimization_barrier((partner, *uppers))
+    early, late = BY_COLUMNS
+    pieces = column_pieces(factors[early])
+    ahead = jnp.stack([piece_for(pieces, rank + step & ranks - 1) for step in (1, 2)])
+    mask_first = masks(block_present[:1])[0]
+    partner, ahead, *uppers = lax.optimization_barrier((partner, ahead, *uppers))
+    forward = [(r, (r + 1) % ranks) for r in range(ranks)]
+    backward = [(r, (r - 1) % ranks) for r in range(ranks)]
+    columns = {}
+
     for level in range(LEVELS):
-        part = product(own, partner, mask[level], weights[level])
         bit = leaf_bits - 2 - level
-        if bit >= 0:
-            received = lax.all_to_all(
-                chunks(part, 2), ("leaf", "rank"), 0, 0, axis_index_groups=pair_groups(leaves, ranks, bit), tiled=True
+        groups = pair_groups(leaves, ranks, bit) if bit >= 0 else None
+        if level in BY_COLUMNS:
+            own = column_product(whole_own, whole_partner, both_masks[level], columns[level], rank)
+            if bit >= 0:
+                partner = lax.ppermute(own.astype(BF16), "leaf", [(at, at ^ 1 << bit) for at in range(leaves)])
+                partner = partner.astype(F32)
+            else:
+                partner = turned(own)
+            continue
+        if level == 0:
+            part = product(own, partner, mask_first, factors[0].reshape(512, 256))
+            part, block_present, factors = lax.optimization_barrier((part, block_present, factors))
+            mask = masks(block_present)
+            weights = factors.reshape(LEVELS, 512, 256)
+            moved = {
+                at: [piece_for(column_pieces(factors[at]), rank + step & ranks - 1) for step in range(ranks)]
+                for at in BY_COLUMNS
+            }
+            both_masks = {at: column_masks(block_present[at]) for at in BY_COLUMNS}
+        else:
+            part = product(own, partner, mask[level], weights[level])
+        if level < 4:
+            if level == 0:
+                first = lax.ppermute(ahead, "rank", forward)
+            elif level == 1:
+                second = lax.ppermute(jnp.stack([moved[early][3], moved[late][2]]), "rank", backward)
+            elif level == 2:
+                third = lax.ppermute(jnp.stack([first[1], moved[late][1]]), "rank", forward)
+            else:
+                fourth = lax.ppermute(jnp.stack([second[1], moved[late][3]]), "rank", backward)
+        if level == 3:
+            part, mine, near, other = lax.optimization_barrier((part, moved[early][0], first[0], second[0]))
+            columns[early] = assembled(mine, near, third[0], other)
+        elif level == 5:
+            part, mine, near, far, other = lax.optimization_barrier(
+                (part, moved[late][0], third[1], fourth[0], fourth[1])
             )
-            upper = uppers[bit]
-            low, high = received[:4].sum(0), received[4:].sum(0)
-            own = jnp.where(upper, high, low)
-            partner = jnp.where(upper, low, high)
+            columns[late] = assembled(mine, near, far, other)
+        if level + 1 in BY_COLUMNS:
+            sent = jnp.broadcast_to(part.astype(WIDE)[None], (2 * ranks, 16, 256))
+            received = lax.all_to_all(sent, ("leaf", "rank"), 0, 0, axis_index_groups=groups, tiled=True)
+            whole_own, whole_partner = by_side(received, uppers[bit])
+        elif bit >= 0:
+            received = lax.all_to_all(chunks(part, 2), ("leaf", "rank"), 0, 0, axis_index_groups=groups, tiled=True)
+            own, partner = by_side(received, uppers[bit])
         elif level < LEVELS - 1:
             own = lax.all_to_all(chunks(part, 1), "rank", 0, 0, tiled=True).sum(0)
             partner = turned(own)
-    whole = lax.all_to_all(jnp.stack([part] * ranks), "rank", 0, 0, tiled=True).sum(0)
+        else:
+            sent = jnp.broadcast_to(part.astype(WIDE)[None], (ranks, 16, 256))
+            whole = lax.all_to_all(sent, "rank", 0, 0, tiled=True).astype(F32).sum(0)
     return put_back(whole, cluster_order)
 
 
@@ -106,4 +185,5 @@
         P(None, "leaf", None, "rank", None),
     )
     out_specs = P("leaf", None, None)
+
     return jax.shard_map(local, mesh=mesh, in_specs=in_specs, out_specs=out_specs, check_vma=False)

time: 155 us -> 146 us (0.942)
  the two profiles are of different devices: /device:TPU:16 before, /device:TPU:56 now
where the time goes in v2:
time: 146 us; the launch traced here: 145 us
  starting transfers between devices  69.7 us (48%)
  waiting for transfers between devices  45.2 us (31%)
  blocking collectives  15.2 us (10%)
  local copies, waits for them, and re-layouts  8.02 us (5%)
  other arithmetic  4.83 us (3%)
  matrix products  1.74 us (1%)
    all_to_all x3, starting transfers between devices, local(): lax.all_to_all(chunks(part, 2), ('leaf', 'rank'), 0, 0, axis_index_groups...  30.9 us
    all_to_all x2, waiting for transfers between devices, local(): lax.all_to_all(sent, ('leaf', 'rank'), 0, 0, axis_index_groups=groups, ti...  28.8 us
    all_to_all x1, blocking collectives, local(): whole = lax.all_to_all(sent, 'rank', 0, 0, tiled=True).astype(F32).sum(0)  15.2 us
    all_to_all x3, waiting for transfers between devices, local(): lax.all_to_all(chunks(part, 2), ('leaf', 'rank'), 0, 0, axis_index_groups...  12.3 us
    all_to_all x2, starting transfers between devices, local(): lax.all_to_all(sent, ('leaf', 'rank'), 0, 0, axis_index_groups=groups, ti...  9.2 us
    ppermute x1, starting transfers between devices, local(): third = lax.ppermute(jnp.stack([first[1], moved[late][1]]), 'rank', forward)  7.83 us
    ppermute x1, starting transfers between devices, local(): first = lax.ppermute(ahead, 'rank', forward)  7.28 us
    ppermute x1, starting transfers between devices, local(): lax.ppermute(jnp.stack([second[1], moved[late][3]]), 'rank', backward)  6.4 us
  transfers between devices with their start and end apart: 11, of which 7 were waited for; matrix products, arithmetic and copies ran while one was open for 6% of the time, Pallas kernels for 0%

profile of v2, /device:TPU:56, one launch (start us, length us, event | category | flops | bytes accessed | tf_op | source)
XLA Modules:
  0.0 145.1 jit_solution(3184758352211536495)
XLA Ops:
  0.0 0.8 constant_dynamic-slice_fusion.6
  0.8 0.2 convolution_bitcast_fusion.1
  1.1 3.1 %collective-permute-start = (bf16[8,128]{1,0:T(8,128)(2,1)S(1)}, bf16[8,128]{1,0:T(8,128)(2,1)S(1)}, u32[]{:S(2)}, u32[]{:S(2)}) collective-permute-start(bf16[8,128]{1,0:T(8,128)(2,1)S(1)} %pad_maximum_fusion.13), channel_id=1, source_target_pairs={{0,256},{4,260},{8,264},{12,268},{16,272},{20,276},{24,280},{28,28... | collective-permute-start | bytes 6152 | tf_op jit(solution)/shard_map/ppermute | solution.py:113
  4.3 1.1 fusion.205
  5.4 0.2 slice_bitcast_fusion.31
  5.6 0.1 fusion.184
  5.7 0.1 maximum_bitcast_fusion.2
  5.8 0.1 maximum_bitcast_fusion
  6.0 0.7 pad_maximum_fusion.5
  6.8 0.1 ne.230
  6.9 1.1 collective-permute-done
  8.2 0.2 fusion.31
  8.4 0.9 fusion.204
  9.4 0.2 fusion.186
  9.7 0.1 copy.24
  9.9 0.6 broadcast_in_dim.49
  10.5 15.7 %all-to-all-start = ((f32[8,8,128]{2,1,0:T(8,128)}), f32[8,8,128]{2,1,0:T(8,128)S(1)}, u32[]{:S(2)}, u32[]{:S(2)}) async-start(f32[8,8,128]{2,1,0:T(8,128)} %bitcast.25), calls=%async_computation | async-start | bytes 65536 | tf_op jit(solution)/shard_map/all_to_all | solution.py:169
  26.2 0.1 slice_bitcast_fusion.23
  26.3 7.3 %collective-permute-start.1 = (bf16[2,4,64,128]{3,2,1,0:T(8,128)(2,1)}, bf16[2,4,64,128]{3,2,1,0:T(8,128)(2,1)S(1)}, u32[]{:S(2)}, u32[]{:S(2)}) collective-permute-start(bf16[2,4,64,128]{3,2,1,0:T(8,128)(2,1)} %pad_maximum_fusion.5), channel_id=1, source_target_pairs={{0,1},{1,2},{2,3},{3,0},{4,5},{5,6},{6,7},{7,4},{8,9},{9,10},{10,1... | collective-permute-start | bytes 393224 | tf_op jit(solution)/shard_map/ppermute | solution.py:149
  33.6 0.2 slice_bitcast_fusion.14
  33.8 0.1 maximum_bitcast_fusion.7
  33.9 0.1 maximum_bitcast_fusion.6
  34.0 0.1 maximum_bitcast_fusion.5
  34.1 0.1 maximum_bitcast_fusion.4
  34.2 0.1 maximum_bitcast_fusion.11
  34.3 0.1 maximum_bitcast_fusion.10
  34.4 0.1 maximum_bitcast_fusion.9
  34.5 0.1 maximum_bitcast_fusion.8
  34.8 2.5 %collective-permute-start.2 = (bf16[2,4,64,128]{3,2,1,0:T(8,128)(2,1)S(1)}, bf16[2,4,64,128]{3,2,1,0:T(8,128)(2,1)S(1)}, u32[]{:S(2)}, u32[]{:S(2)}) collective-permute-start(bf16[2,4,64,128]{3,2,1,0:T(8,128)(2,1)S(1)} %pad_maximum_fusion.6), channel_id=1, source_target_pairs={{0,3},{1,0},{2,1},{3,2},{4,7},{5,4},{6,5},{7,6},{8,11},{9,8},{10,9... | collective-permute-start | bytes 393224 | tf_op jit(solution)/shard_map/ppermute | solution.py:151
  37.3 0.1 ne.243
  37.5 0.1 ne.240
  37.6 0.1 select_convert_fusion
  37.7 0.1 compare_and_fusion
  37.8 0.7 all-to-all-done
  38.8 0.1 fusion.52
  39.1 0.6 broadcast_in_dim.53
  39.8 10.7 %all-to-all-start.1 = ((f32[8,8,128]{2,1,0:T(8,128)}), f32[8,8,128]{2,1,0:T(8,128)S(1)}, u32[]{:S(2)}, u32[]{:S(2)}) async-start(f32[8,8,128]{2,1,0:T(8,128)} %bitcast.35), calls=%async_computation.1 | async-start | bytes 65536 | tf_op jit(solution)/shard_map/all_to_all | solution.py:169
  50.6 7.8 %collective-permute-start.3 = (bf16[2,4,64,128]{3,2,1,0:T(8,128)(2,1)S(1)}, bf16[2,4,64,128]{3,2,1,0:T(8,128)(2,1)S(1)}, u32[]{:S(2)}, u32[]{:S(2)}) collective-permute-start(bf16[2,4,64,128]{3,2,1,0:T(8,128)(2,1)S(1)} %pad_maximum_fusion.7), channel_id=1, source_target_pairs={{0,1},{1,2},{2,3},{3,0},{4,5},{5,6},{6,7},{7,4},{8,9},{9,10},{10,1... | collective-permute-start | bytes 393224 | tf_op jit(solution)/shard_map/ppermute | solution.py:153
  58.4 5.7 %all-to-all-done.1 = f32[8,8,128]{2,1,0:T(8,128)S(1)} async-done(((f32[8,8,128]{2,1,0:T(8,128)}), f32[8,8,128]{2,1,0:T(8,128)S(1)}, u32[]{:S(2)}, u32[]{:S(2)}) %all-to-all-start.1) | async-done | bytes 32800 | tf_op jit(solution)/shard_map/all_to_all | solution.py:169
  64.5 0.1 fusion.49
  64.8 0.6 broadcast_in_dim.54
  65.4 4.5 %all-to-all-start.2 = ((f32[8,8,128]{2,1,0:T(8,128)}), f32[8,8,128]{2,1,0:T(8,128)S(1)}, u32[]{:S(2)}, u32[]{:S(2)}) async-start(f32[8,8,128]{2,1,0:T(8,128)} %bitcast.44), calls=%async_computation.2 | async-start | bytes 65536 | tf_op jit(solution)/shard_map/all_to_all | solution.py:169
  69.9 6.4 %collective-permute-start.5 = (bf16[2,4,64,128]{3,2,1,0:T(8,128)(2,1)S(1)}, bf16[2,4,64,128]{3,2,1,0:T(8,128)(2,1)S(1)}, u32[]{:S(2)}, u32[]{:S(2)}) collective-permute-start(bf16[2,4,64,128]{3,2,1,0:T(8,128)(2,1)S(1)} %pad_maximum_fusion.8), channel_id=1, source_target_pairs={{0,3},{1,0},{2,1},{3,2},{4,7},{5,4},{6,5},{7,6},{8,11},{9,8},{10,9... | collective-permute-start | bytes 393224 | tf_op jit(solution)/shard_map/ppermute | solution.py:155
  76.3 5.8 %all-to-all-done.2 = f32[8,8,128]{2,1,0:T(8,128)S(1)} async-done(((f32[8,8,128]{2,1,0:T(8,128)}), f32[8,8,128]{2,1,0:T(8,128)S(1)}, u32[]{:S(2)}, u32[]{:S(2)}) %all-to-all-start.2) | async-done | bytes 32800 | tf_op jit(solution)/shard_map/all_to_all | solution.py:169
  82.4 0.1 fusion.46
  82.6 0.6 broadcast_in_dim.55
  83.2 5.9 %all-to-all-start.3 = ((bf16[8,16,256]{2,1,0:T(8,128)(2,1)}), bf16[8,16,256]{2,1,0:T(8,128)(2,1)S(1)}, u32[]{:S(2)}, u32[]{:S(2)}) async-start(bf16[8,16,256]{2,1,0:T(8,128)(2,1)} %broadcast_in_dim.55), calls=%async_computation.3 | async-start | bytes 131072 | tf_op jit(solution)/shard_map/all_to_all | solution.py:166
  89.1 15.7 %all-to-all-done.3 = bf16[8,16,256]{2,1,0:T(8,128)(2,1)S(1)} async-done(((bf16[8,16,256]{2,1,0:T(8,128)(2,1)}), bf16[8,16,256]{2,1,0:T(8,128)(2,1)S(1)}, u32[]{:S(2)}, u32[]{:S(2)}) %all-to-all-start.3) | async-done | bytes 65568 | tf_op jit(solution)/shard_map/all_to_all | solution.py:166
  104.9 0.1 fusion.37
  105.1 0.2 fusion.5
  105.2 0.1 slice_add_fusion.3
  105.4 2.5 %collective-permute-start.4 = (bf16[8,128]{1,0:T(8,128)(2,1)S(1)}, bf16[8,128]{1,0:T(8,128)(2,1)S(1)}, u32[]{:S(2)}, u32[]{:S(2)}) collective-permute-start(bf16[8,128]{1,0:T(8,128)(2,1)S(1)} %fusion.187), channel_id=1, source_target_pairs={{0,8},{4,12},{8,0},{12,4},{16,24},{20,28},{24,16},{28,20},{32,40},... | collective-permute-start | bytes 6152 | tf_op jit(solution)/shard_map/ppermute | solution.py:130
  107.9 2.9 %collective-permute-done.4 = bf16[8,128]{1,0:T(8,128)(2,1)S(1)} collective-permute-done((bf16[8,128]{1,0:T(8,128)(2,1)S(1)}, bf16[8,128]{1,0:T(8,128)(2,1)S(1)}, u32[]{:S(2)}, u32[]{:S(2)}) %collective-permute-start.4) | collective-permute-done | bytes 2080 | tf_op jit(solution)/shard_map/ppermute | solution.py:130
  111.0 0.1 fusion.43
  111.2 0.6 broadcast_in_dim.103
  111.8 3.3 %all-to-all-start.4 = ((bf16[8,16,256]{2,1,0:T(8,128)(2,1)}), bf16[8,16,256]{2,1,0:T(8,128)(2,1)S(1)}, u32[]{:S(2)}, u32[]{:S(2)}) async-start(bf16[8,16,256]{2,1,0:T(8,128)(2,1)} %broadcast_in_dim.103), calls=%async_computation.4 | async-start | bytes 131072 | tf_op jit(solution)/shard_map/all_to_all | solution.py:166
  115.2 13.1 %all-to-all-done.4 = bf16[8,16,256]{2,1,0:T(8,128)(2,1)S(1)} async-done(((bf16[8,16,256]{2,1,0:T(8,128)(2,1)}), bf16[8,16,256]{2,1,0:T(8,128)(2,1)S(1)}, u32[]{:S(2)}, u32[]{:S(2)}) %all-to-all-start.4) | async-done | bytes 65568 | tf_op jit(solution)/shard_map/all_to_all | solution.py:166
  128.3 0.1 fusion.34
  128.5 0.2 fusion.8
  128.6 0.1 slice_add_fusion.2
  128.8 0.2 convolution_convert_fusion
  129.0 15.2 %all_to_all.30 = bf16[4,16,256]{2,1,0:T(8,128)(2,1)S(1)} all-to-all(bf16[4,16,256]{2,1,0:T(8,128)(2,1)S(1)} %broadcast_in_dim.105), channel_id=1, replica_groups=mesh['leaf'=128,'rank'=4] {'rank'}, dimensions={0} | all-to-all | bytes 65536 | tf_op jit(solution)/shard_map/all_to_all | solution.py:176
  144.2 0.3 convolution_bitcast_fusion
  144.5 0.6 fusion.39
  (92 shorter events, 2.9 us)
Async XLA Ops:
  0.0 0.8 copy-start
  0.0 5.6 %copy-start.4 = (s32[8,4]{0,1:T(4,128)S(1)}, s32[8,4]{0,1:T(4,128)}, u32[]{:S(2)}) copy-start(s32[8,4]{0,1:T(4,128)} %param.6) | copy-start | bytes 388
  1.1 7.0 %collective-permute-start = (bf16[8,128]{1,0:T(8,128)(2,1)S(1)}, bf16[8,128]{1,0:T(8,128)(2,1)S(1)}, u32[]{:S(2)}, u32[]{:S(2)}) collective-permute-start(bf16[8,128]{1,0:T(8,128)(2,1)S(1)} %pad_maximum_fusion.13), channel_id=1, source_target_pairs={{0,256},{4,260},{8,264},{12,268},{16,272},{20,276},{24,280},{28,28... | collective-permute-start | bytes 6152 | tf_op jit(solution)/shard_map/ppermute | solution.py:113
  5.4 3.1 %copy-start.1 = (bf16[8,4,2,64,256]{4,3,2,1,0:T(8,128)(2,1)S(1)}, bf16[8,4,2,64,256]{4,3,2,1,0:T(8,128)(2,1)}, u32[]{:S(2)}) copy-start(bf16[8,4,2,64,256]{4,3,2,1,0:T(8,128)(2,1)} %param.7) | copy-start | bytes 6291460
  10.5 28.0 %all-to-all-start = ((f32[8,8,128]{2,1,0:T(8,128)}), f32[8,8,128]{2,1,0:T(8,128)S(1)}, u32[]{:S(2)}, u32[]{:S(2)}) async-start(f32[8,8,128]{2,1,0:T(8,128)} %bitcast.25), calls=%async_computation | async-start | bytes 65536 | tf_op jit(solution)/shard_map/all_to_all | solution.py:169
  26.3 24.2 %collective-permute-start.1 = (bf16[2,4,64,128]{3,2,1,0:T(8,128)(2,1)}, bf16[2,4,64,128]{3,2,1,0:T(8,128)(2,1)S(1)}, u32[]{:S(2)}, u32[]{:S(2)}) collective-permute-start(bf16[2,4,64,128]{3,2,1,0:T(8,128)(2,1)} %pad_maximum_fusion.5), channel_id=1, source_target_pairs={{0,1},{1,2},{2,3},{3,0},{4,5},{5,6},{6,7},{7,4},{8,9},{9,10},{10,1... | collective-permute-start | bytes 393224 | tf_op jit(solution)/shard_map/ppermute | solution.py:149
  33.8 5.1 %copy-start.3 = (bf16[1,4,2,64,256]{4,3,2,1,0:T(8,128)(2,1)S(1)}, bf16[1,4,2,64,256]{4,3,2,1,0:T(8,128)(2,1)}, u32[]{:S(2)}) copy-start(bf16[1,4,2,64,256]{4,3,2,1,0:T(8,128)(2,1)} %get-tuple-element.63) | copy-start | bytes 786436
  34.5 30.0 %copy-start.2 = (bf16[1,4,2,64,256]{4,3,2,1,0:T(8,128)(2,1)S(1)}, bf16[1,4,2,64,256]{4,3,2,1,0:T(8,128)(2,1)}, u32[]{:S(2)}) copy-start(bf16[1,4,2,64,256]{4,3,2,1,0:T(8,128)(2,1)} %get-tuple-element.67) | copy-start | bytes 786436
  34.8 23.6 %collective-permute-start.2 = (bf16[2,4,64,128]{3,2,1,0:T(8,128)(2,1)S(1)}, bf16[2,4,64,128]{3,2,1,0:T(8,128)(2,1)S(1)}, u32[]{:S(2)}, u32[]{:S(2)}) collective-permute-start(bf16[2,4,64,128]{3,2,1,0:T(8,128)(2,1)S(1)} %pad_maximum_fusion.6), channel_id=1, source_target_pairs={{0,3},{1,0},{2,1},{3,2},{4,7},{5,4},{6,5},{7,6},{8,11},{9,8},{10,9... | collective-permute-start | bytes 393224 | tf_op jit(solution)/shard_map/ppermute | solution.py:151
  39.8 24.4 %all-to-all-start.1 = ((f32[8,8,128]{2,1,0:T(8,128)}), f32[8,8,128]{2,1,0:T(8,128)S(1)}, u32[]{:S(2)}, u32[]{:S(2)}) async-start(f32[8,8,128]{2,1,0:T(8,128)} %bitcast.35), calls=%async_computation.1 | async-start | bytes 65536 | tf_op jit(solution)/shard_map/all_to_all | solution.py:169
  50.6 38.5 %collective-permute-start.3 = (bf16[2,4,64,128]{3,2,1,0:T(8,128)(2,1)S(1)}, bf16[2,4,64,128]{3,2,1,0:T(8,128)(2,1)S(1)}, u32[]{:S(2)}, u32[]{:S(2)}) collective-permute-start(bf16[2,4,64,128]{3,2,1,0:T(8,128)(2,1)S(1)} %pad_maximum_fusion.7), channel_id=1, source_target_pairs={{0,1},{1,2},{2,3},{3,0},{4,5},{5,6},{6,7},{7,4},{8,9},{9,10},{10,1... | collective-permute-start | bytes 393224 | tf_op jit(solution)/shard_map/ppermute | solution.py:153
  65.4 16.7 %all-to-all-start.2 = ((f32[8,8,128]{2,1,0:T(8,128)}), f32[8,8,128]{2,1,0:T(8,128)S(1)}, u32[]{:S(2)}, u32[]{:S(2)}) async-start(f32[8,8,128]{2,1,0:T(8,128)} %bitcast.44), calls=%async_computation.2 | async-start | bytes 65536 | tf_op jit(solution)/shard_map/all_to_all | solution.py:169
  69.9 38.0 %collective-permute-start.5 = (bf16[2,4,64,128]{3,2,1,0:T(8,128)(2,1)S(1)}, bf16[2,4,64,128]{3,2,1,0:T(8,128)(2,1)S(1)}, u32[]{:S(2)}, u32[]{:S(2)}) collective-permute-start(bf16[2,4,64,128]{3,2,1,0:T(8,128)(2,1)S(1)} %pad_maximum_fusion.8), channel_id=1, source_target_pairs={{0,3},{1,0},{2,1},{3,2},{4,7},{5,4},{6,5},{7,6},{8,11},{9,8},{10,9... | collective-permute-start | bytes 393224 | tf_op jit(solution)/shard_map/ppermute | solution.py:155
  83.2 21.7 %all-to-all-start.3 = ((bf16[8,16,256]{2,1,0:T(8,128)(2,1)}), bf16[8,16,256]{2,1,0:T(8,128)(2,1)S(1)}, u32[]{:S(2)}, u32[]{:S(2)}) async-start(bf16[8,16,256]{2,1,0:T(8,128)(2,1)} %broadcast_in_dim.55), calls=%async_computation.3 | async-start | bytes 131072 | tf_op jit(solution)/shard_map/all_to_all | solution.py:166
  89.1 55.1 %copy-start.5 = (s32[4,256]{1,0:T(4,128)S(1)}, s32[4,256]{1,0:T(4,128)}, u32[]{:S(2)}) copy-start(s32[4,256]{1,0:T(4,128)} %param.5) | copy-start | bytes 12292
  105.4 5.5 %collective-permute-start.4 = (bf16[8,128]{1,0:T(8,128)(2,1)S(1)}, bf16[8,128]{1,0:T(8,128)(2,1)S(1)}, u32[]{:S(2)}, u32[]{:S(2)}) collective-permute-start(bf16[8,128]{1,0:T(8,128)(2,1)S(1)} %fusion.187), channel_id=1, source_target_pairs={{0,8},{4,12},{8,0},{12,4},{16,24},{20,28},{24,16},{28,20},{32,40},... | collective-permute-start | bytes 6152 | tf_op jit(solution)/shard_map/ppermute | solution.py:130
  111.8 16.5 %all-to-all-start.4 = ((bf16[8,16,256]{2,1,0:T(8,128)(2,1)}), bf16[8,16,256]{2,1,0:T(8,128)(2,1)S(1)}, u32[]{:S(2)}, u32[]{:S(2)}) async-start(bf16[8,16,256]{2,1,0:T(8,128)(2,1)} %broadcast_in_dim.103), calls=%async_computation.4 | async-start | bytes 131072 | tf_op jit(solution)/shard_map/all_to_all | solution.py:166

commit v3 on v2

v3 whole, which is shorter than its diff:
```python
import jax
import jax.numpy as jnp
from jax import lax
from jax.sharding import PartitionSpec as P

LEVELS = 8
F32 = jnp.float32
BF16 = jnp.bfloat16
WIDE = BF16
BY_COLUMNS = (3, 6)


def left_half():
    return lax.broadcasted_iota(jnp.int32, (8, 128), 1) < 64


def turned(tile):
    return jnp.concatenate([tile[:, 64:], tile[:, :64]], axis=1)


def own_columns(loads, order, rank):
    quarter = lax.dynamic_slice_in_dim(order, 64 * rank, 64, 1)
    pick = (jnp.arange(256)[None, :, None] == quarter[:, None, :]).astype(BF16)
    got = jnp.einsum("blc,bco->blo", loads, pick, preferred_element_type=F32)
    return jnp.concatenate([got[:2].reshape(8, 64), got[2:].reshape(8, 64)], axis=1)


def per_block(wide):
    _, columns = wide.shape
    block_of = lax.broadcasted_iota(jnp.int32, wide.shape, 0) // 4 % 4
    part_of = lax.broadcasted_iota(jnp.int32, wide.shape, 1) // (columns // 4)
    return jnp.where(block_of == part_of, wide, jnp.zeros((), wide.dtype))


def product(own, partner, present, weights):
    left = left_half()
    partner = partner * present
    top = jnp.where(left, own, turned(partner))
    bottom = jnp.where(left, turned(own), partner)
    cols = jnp.concatenate([top, bottom], axis=0).astype(BF16)
    wide = per_block(jnp.concatenate([cols] * 4, axis=1))
    return jnp.dot(wide, weights, preferred_element_type=F32)


def chunks(part, copies):
    left = left_half()
    pieces = []
    for at in range(2):
        tile = part[:, 128 * at : 128 * (at + 1)]
        top, bottom = tile[:8], tile[8:]
        pieces += [jnp.where(left, top, turned(bottom)), jnp.where(left, turned(top), bottom)]
    return jnp.broadcast_to(jnp.stack(pieces)[None], (copies, 4, 8, 128)).reshape(copies * 4, 8, 128)


def put_back(state, order):
    high = state.astype(BF16)
    rest = state - high.astype(F32)
    middle = rest.astype(BF16)
    low = (rest - middle.astype(F32)).astype(BF16)
    pieces = jnp.concatenate([high, middle, low], axis=0).reshape(3, 4, 4, 256)
    pick = (jnp.arange(256)[None, :, None] == order[:, None, :]).astype(BF16)
    put = jnp.einsum("pblj,bij->pbli", pieces, pick, preferred_element_type=F32)
    return put[0] + put[1] + put[2]


def pair_groups(leaves, ranks, bit):
    groups = []
    for leaf in range(leaves):
        if not leaf >> bit & 1:
            groups.append([at * ranks + r for at in (leaf, leaf | 1 << bit) for r in range(ranks)])
    return groups


def present_tiles(present):
    levels = present.shape[0]
    spread = present.reshape(levels, 2, 2).transpose(0, 2, 1).astype(F32)
    return jnp.broadcast_to(spread[:, :, None, :, None], (levels, 2, 4, 2, 64)).reshape(levels, 8, 128)


def piece_for(pieces, quarter):
    return lax.dynamic_index_in_dim(pieces, quarter, 0, keepdims=False)


def column_pieces(weights):
    parts = [jnp.concatenate([weights[:, 0, :, 64 * q : 64 * q + 64], weights[:, 1, :, 64 * q : 64 * q + 64]], 2) for q in range(4)]
    return jnp.stack(parts)


def assembled(mine, first, second, far, first_is_next):
    after, before = jnp.where(first_is_next, first, second), jnp.where(first_is_next, second, first)
    return jnp.stack([mine, after, far, before], axis=1).reshape(1024, 128)


def column_product(own, partner, present, columns, rank):
    partner = partner * jnp.repeat(present.astype(F32), 4)[:, None]
    both = jnp.concatenate([own, partner], axis=0).astype(BF16)
    turn = lax.dynamic_slice_in_dim(jnp.concatenate([both, both], axis=1), 64 * rank, 256, 1)
    got = jnp.dot(per_block(jnp.concatenate([turn] * 4, axis=1)), columns, preferred_element_type=F32)
    got = got[:16, :64] + got[16:, 64:]
    return jnp.concatenate([got[:8], got[8:]], axis=1)


def by_side(received, upper):
    low, high = received[:4].astype(F32).sum(0), received[4:].astype(F32).sum(0)
    return jnp.where(upper, high, low), jnp.where(upper, low, high)


def local(load_vectors, cluster_order, block_present, factors):
    leaves, ranks = lax.axis_size("leaf"), lax.axis_size("rank")
    leaf_bits = leaves.bit_length() - 1
    leaf, rank = lax.axis_index("leaf"), lax.axis_index("rank")
    own = own_columns(load_vectors, cluster_order, rank)
    partner = lax.ppermute(own, "leaf", [(at, at ^ 1 << leaf_bits - 1) for at in range(leaves)])
    uppers = [(leaf >> bit & 1) != 0 for bit in range(leaf_bits - 1)]
    core = leaf & 1
    steps = (jnp.where(core == 0, rank ^ 1, 3 - rank), jnp.where(core == 0, 3 - rank, rank ^ 1))

    def moved_on(pieces, step):
        route = []
        for at in range(leaves):
            for r in range(ranks):
                route.append((at * ranks + r, at * ranks + (r ^ 1 if at & 1 == step else 3 - r)))
        return lax.ppermute(jnp.stack(pieces), ("leaf", "rank"), route)

    early, late = BY_COLUMNS
    pieces = {level: column_pieces(factors[level]) for level in BY_COLUMNS}
    moved = [piece_for(pieces[level], to) for level in BY_COLUMNS for to in (rank, *steps, rank ^ 2)]
    first_is_next = (rank + core & 1) == 0
    tiles = present_tiles(block_present)
    partner, tiles, block_present, *rest = lax.optimization_barrier((partner, tiles, block_present, *moved, *uppers))
    of_early, of_late, uppers = rest[:ranks], rest[ranks : 2 * ranks], rest[2 * ranks :]
    columns = {}

    for level in range(LEVELS):
        bit = leaf_bits - 2 - level
        groups = pair_groups(leaves, ranks, bit) if bit >= 0 else None
        if level == early:
            second, whole_own, whole_partner = lax.optimization_barrier((second, whole_own, whole_partner))
            columns[early] = assembled(of_early[0], first[0], second[0], second[1], first_is_next)
        elif level == late:
            third, whole_own, whole_partner = lax.optimization_barrier((third, whole_own, whole_partner))
            columns[late] = assembled(of_late[0], first[2], third[0], third[1], first_is_next)
        if level in BY_COLUMNS:
            own = column_product(whole_own, whole_partner, block_present[level], columns[level], rank)
            if bit >= 0:
                partner = lax.ppermute(own.astype(BF16), "leaf", [(at, at ^ 1 << bit) for at in range(leaves)])
                partner = partner.astype(F32)
            else:
                partner = turned(own)
            continue
        part, factors = lax.optimization_barrier(
            (product(own, partner, tiles[level], factors[level].reshape(512, 256)), factors)
        )
        if level == 0:
            first = moved_on([of_early[1], of_early[3], of_late[1], of_late[3]], 0)
        elif level == 1:
            second = moved_on([of_early[2], first[1]], 1)
        elif level == 4:
            third = moved_on([of_late[2], first[3]], 1)
        if level + 1 in BY_COLUMNS:
            sent = jnp.broadcast_to(part.astype(WIDE)[None], (2 * ranks, 16, 256))
            received = lax.all_to_all(sent, ("leaf", "rank"), 0, 0, axis_index_groups=groups, tiled=True)
            whole_own, whole_partner = by_side(received, uppers[bit])
        elif bit >= 0:
            received = lax.all_to_all(chunks(part, 2), ("leaf", "rank"), 0, 0, axis_index_groups=groups, tiled=True)
            own, partner = by_side(received, uppers[bit])
        elif level < LEVELS - 1:
            own = lax.all_to_all(chunks(part, 1), "rank", 0, 0, tiled=True).sum(0)
            partner = turned(own)
        else:
            sent = jnp.broadcast_to(part.astype(WIDE)[None], (ranks, 16, 256))
            whole = lax.all_to_all(sent, "rank", 0, 0, tiled=True).astype(F32).sum(0)
    return put_back(whole, cluster_order)


def solution(mesh):
    in_specs = (
        P("leaf", None, None),
        P("leaf", None),
        P(None, "leaf"),
        P(None, "leaf", None, "rank", None),
    )
    out_specs = P("leaf", None, None)

    return jax.shard_map(local, mesh=mesh, in_specs=in_specs, out_specs=out_specs, check_vma=False)
```

time: 146 us -> 160 us (1.096)
  the two profiles are of different devices: /device:TPU:56 before, /device:TPU:4 now
where the time goes in v3:
time: 160 us; the launch traced here: 159 us
  starting transfers between devices  70.7 us (44%)
  waiting for transfers between devices  47.8 us (30%)
  blocking collectives  26.9 us (17%)
  local copies, waits for them, and re-layouts  6.94 us (4%)
  other arithmetic  4.02 us (3%)
  matrix products  2.11 us (1%)
    all_to_all x3, waiting for transfers between devices, local(): lax.all_to_all(chunks(part, 2), ('leaf', 'rank'), 0, 0, axis_index_groups...  31.7 us
    all_to_all x3, starting transfers between devices, local(): lax.all_to_all(chunks(part, 2), ('leaf', 'rank'), 0, 0, axis_index_groups...  27.6 us
    all_to_all x1, blocking collectives, local(): whole = lax.all_to_all(sent, 'rank', 0, 0, tiled=True).astype(F32).sum(0)  26.9 us
    ppermute x3, starting transfers between devices, moved_on(): return lax.ppermute(jnp.stack(pieces), ('leaf', 'rank'), route)  23.3 us
    all_to_all x2, starting transfers between devices, local(): lax.all_to_all(sent, ('leaf', 'rank'), 0, 0, axis_index_groups=groups, ti...  12.3 us
    all_to_all x2, waiting for transfers between devices, local(): lax.all_to_all(sent, ('leaf', 'rank'), 0, 0, axis_index_groups=groups, ti...  9.4 us
    ppermute x1, starting transfers between devices, local(): lax.ppermute(own, 'leaf', [(at, at ^ 1 << leaf_bits - 1) for at in range(...  5.1 us
    ppermute x1, waiting for transfers between devices, local(): lax.ppermute(own.astype(BF16), 'leaf', [(at, at ^ 1 << bit) for at in ran...  4.56 us
  transfers between devices with their start and end apart: 10, of which 7 were waited for; matrix products, arithmetic and copies ran while one was open for 3% of the time, Pallas kernels for 0%

profile of v3, /device:TPU:4, one launch (start us, length us, event | category | flops | bytes accessed | tf_op | source)
XLA Modules:
  0.0 159.0 jit_solution(2639940065455730864)
XLA Ops:
  0.0 0.8 constant_dynamic-slice_fusion
  0.8 0.2 convolution_bitcast_fusion.1
  1.1 5.1 %collective-permute-start = (f32[8,128]{1,0:T(8,128)S(1)}, f32[8,128]{1,0:T(8,128)S(1)}, u32[]{:S(2)}, u32[]{:S(2)}) collective-permute-start(f32[8,128]{1,0:T(8,128)S(1)} %pad_maximum_fusion.11), channel_id=1, source_target_pairs={{0,256},{4,260},{8,264},{12,268},{16,272},{20,276},{24,280},{28,28... | collective-permute-start | bytes 12296 | tf_op jit(solution)/shard_map/ppermute | solution.py:113
  6.3 1.2 slice_bitcast_fusion
  7.4 0.3 slice_bitcast_fusion.9
  7.7 0.1 maximum_bitcast_fusion.4
  7.8 0.1 maximum_bitcast_fusion.5
  7.9 0.1 maximum_bitcast_fusion.6
  8.0 0.1 maximum_bitcast_fusion.7
  8.1 0.1 maximum_bitcast_fusion
  8.2 0.1 maximum_bitcast_fusion.1
  8.3 0.1 maximum_bitcast_fusion.2
  8.4 0.1 maximum_bitcast_fusion.3
  8.8 0.1 copy.39
  8.9 0.1 broadcast_in_dim.32
  8.9 0.1 reshape.122
  9.2 0.1 fusion.131
  9.3 0.2 fusion.32
  9.6 0.1 fusion.133
  9.6 0.6 broadcast_in_dim.34
  10.3 15.2 %all-to-all-start = ((f32[8,8,128]{2,1,0:T(8,128)}), f32[8,8,128]{2,1,0:T(8,128)S(1)}, u32[]{:S(2)}, u32[]{:S(2)}) async-start(f32[8,8,128]{2,1,0:T(8,128)} %bitcast.53), calls=%async_computation | async-start | bytes 65536 | tf_op jit(solution)/shard_map/all_to_all | solution.py:165
  25.5 13.4 %all-to-all-done = f32[8,8,128]{2,1,0:T(8,128)S(1)} async-done(((f32[8,8,128]{2,1,0:T(8,128)}), f32[8,8,128]{2,1,0:T(8,128)S(1)}, u32[]{:S(2)}, u32[]{:S(2)}) %all-to-all-start) | async-done | bytes 32800 | tf_op jit(solution)/shard_map/all_to_all | solution.py:165
  39.0 0.1 fusion.137
  39.2 0.1 fusion.138
  39.3 0.2 fusion.47
  39.5 0.1 fusion.139
  39.6 0.6 broadcast_in_dim.35
  40.2 3.3 %all-to-all-start.1 = ((f32[8,8,128]{2,1,0:T(8,128)}), f32[8,8,128]{2,1,0:T(8,128)S(1)}, u32[]{:S(2)}, u32[]{:S(2)}) async-start(f32[8,8,128]{2,1,0:T(8,128)} %bitcast.60), calls=%async_computation.1 | async-start | bytes 65536 | tf_op jit(solution)/shard_map/all_to_all | solution.py:165
  43.6 7.7 %collective-permute-start.1 = (bf16[4,4,64,128]{3,2,1,0:T(8,128)(2,1)S(1)}, bf16[4,4,64,128]{3,2,1,0:T(8,128)(2,1)S(1)}, u32[]{:S(2)}, u32[]{:S(2)}) collective-permute-start(bf16[4,4,64,128]{3,2,1,0:T(8,128)(2,1)S(1)} %pad_maximum_fusion.2), channel_id=1, source_target_pairs={{0,1},{1,0},{2,3},{3,2},{4,7},{5,6},{6,5},{7,4},{8,9},{9,8},{10,11... | collective-permute-start | bytes 786440 | tf_op jit(solution)/shard_map/ppermute | solution.py:123
  51.4 4.7 %all-to-all-done.1 = f32[8,8,128]{2,1,0:T(8,128)S(1)} async-done(((f32[8,8,128]{2,1,0:T(8,128)}), f32[8,8,128]{2,1,0:T(8,128)S(1)}, u32[]{:S(2)}, u32[]{:S(2)}) %all-to-all-start.1) | async-done | bytes 32800 | tf_op jit(solution)/shard_map/all_to_all | solution.py:165
  56.4 0.2 fusion.62
  56.6 0.6 broadcast_in_dim.36
  57.2 9.0 %all-to-all-start.2 = ((bf16[8,16,256]{2,1,0:T(8,128)(2,1)}), bf16[8,16,256]{2,1,0:T(8,128)(2,1)S(1)}, u32[]{:S(2)}, u32[]{:S(2)}) async-start(bf16[8,16,256]{2,1,0:T(8,128)(2,1)} %broadcast_in_dim.36), calls=%async_computation.2 | async-start | bytes 131072 | tf_op jit(solution)/shard_map/all_to_all | solution.py:162
  66.2 0.2 convert_reduce_fusion.5
  66.5 0.1 mul.47
  66.6 7.8 %collective-permute-start.3 = (bf16[2,4,64,128]{3,2,1,0:T(8,128)(2,1)S(1)}, bf16[2,4,64,128]{3,2,1,0:T(8,128)(2,1)S(1)}, u32[]{:S(2)}, u32[]{:S(2)}) collective-permute-start(bf16[2,4,64,128]{3,2,1,0:T(8,128)(2,1)S(1)} %pad_maximum_fusion.6), channel_id=1, source_target_pairs={{0,3},{1,2},{2,1},{3,0},{4,5},{5,4},{6,7},{7,6},{8,11},{9,10},{10,... | collective-permute-start | bytes 393224 | tf_op jit(solution)/shard_map/ppermute | solution.py:123
  74.5 4.6 %all-to-all-done.2 = bf16[8,16,256]{2,1,0:T(8,128)(2,1)S(1)} async-done(((bf16[8,16,256]{2,1,0:T(8,128)(2,1)}), bf16[8,16,256]{2,1,0:T(8,128)(2,1)S(1)}, u32[]{:S(2)}, u32[]{:S(2)}) %all-to-all-start.2) | async-done | bytes 65568 | tf_op jit(solution)/shard_map/all_to_all | solution.py:162
  79.1 2.2 %collective-permute-done.3 = bf16[2,4,64,128]{3,2,1,0:T(8,128)(2,1)S(1)} collective-permute-done((bf16[2,4,64,128]{3,2,1,0:T(8,128)(2,1)S(1)}, bf16[2,4,64,128]{3,2,1,0:T(8,128)(2,1)S(1)}, u32[]{:S(2)}, u32[]{:S(2)}) %collective-permute-start.3) | collective-permute-done | bytes 131104 | tf_op jit(solution)/shard_map/ppermute | solution.py:123
  81.3 0.1 fusion.29
  81.5 0.2 fusion.6
  81.8 0.1 slice_add_fusion.3
  81.9 2.4 %collective-permute-start.4 = (bf16[8,128]{1,0:T(8,128)(2,1)S(1)}, bf16[8,128]{1,0:T(8,128)(2,1)S(1)}, u32[]{:S(2)}, u32[]{:S(2)}) collective-permute-start(bf16[8,128]{1,0:T(8,128)(2,1)S(1)} %fusion.158), channel_id=1, source_target_pairs={{0,16},{4,20},{8,24},{12,28},{16,0},{20,4},{24,8},{28,12},{32,48},... | collective-permute-start | bytes 6152 | tf_op jit(solution)/shard_map/ppermute | solution.py:146
  84.4 4.6 %collective-permute-done.4 = bf16[8,128]{1,0:T(8,128)(2,1)S(1)} collective-permute-done((bf16[8,128]{1,0:T(8,128)(2,1)S(1)}, bf16[8,128]{1,0:T(8,128)(2,1)S(1)}, u32[]{:S(2)}, u32[]{:S(2)}) %collective-permute-start.4) | collective-permute-done | bytes 2080 | tf_op jit(solution)/shard_map/ppermute | solution.py:146
  89.1 0.1 fusion.145
  89.2 0.2 fusion.77
  89.4 0.1 fusion.147
  89.5 0.6 broadcast_in_dim.73
  90.1 9.1 %all-to-all-start.3 = ((f32[8,8,128]{2,1,0:T(8,128)}), f32[8,8,128]{2,1,0:T(8,128)S(1)}, u32[]{:S(2)}, u32[]{:S(2)}) async-start(f32[8,8,128]{2,1,0:T(8,128)} %bitcast.76), calls=%async_computation.3 | async-start | bytes 65536 | tf_op jit(solution)/shard_map/all_to_all | solution.py:165
  99.2 13.5 %all-to-all-done.3 = f32[8,8,128]{2,1,0:T(8,128)S(1)} async-done(((f32[8,8,128]{2,1,0:T(8,128)}), f32[8,8,128]{2,1,0:T(8,128)S(1)}, u32[]{:S(2)}, u32[]{:S(2)}) %all-to-all-start.3) | async-done | bytes 32800 | tf_op jit(solution)/shard_map/all_to_all | solution.py:165
  113.0 0.2 fusion.92
  113.2 0.6 broadcast_in_dim.74
  113.8 3.3 %all-to-all-start.4 = ((bf16[8,16,256]{2,1,0:T(8,128)(2,1)}), bf16[8,16,256]{2,1,0:T(8,128)(2,1)S(1)}, u32[]{:S(2)}, u32[]{:S(2)}) async-start(bf16[8,16,256]{2,1,0:T(8,128)(2,1)} %broadcast_in_dim.74), calls=%async_computation.4 | async-start | bytes 131072 | tf_op jit(solution)/shard_map/all_to_all | solution.py:162
  117.3 0.1 mul.52
  117.4 7.7 %collective-permute-start.2 = (bf16[2,4,64,128]{3,2,1,0:T(8,128)(2,1)S(1)}, bf16[2,4,64,128]{3,2,1,0:T(8,128)(2,1)S(1)}, u32[]{:S(2)}, u32[]{:S(2)}) collective-permute-start(bf16[2,4,64,128]{3,2,1,0:T(8,128)(2,1)S(1)} %pad_maximum_fusion.5), channel_id=1, source_target_pairs={{0,3},{1,2},{2,1},{3,0},{4,5},{5,4},{6,7},{7,6},{8,11},{9,10},{10,... | collective-permute-start | bytes 393224 | tf_op jit(solution)/shard_map/ppermute | solution.py:123
  125.1 4.8 %all-to-all-done.4 = bf16[8,16,256]{2,1,0:T(8,128)(2,1)S(1)} async-done(((bf16[8,16,256]{2,1,0:T(8,128)(2,1)}), bf16[8,16,256]{2,1,0:T(8,128)(2,1)S(1)}, u32[]{:S(2)}, u32[]{:S(2)}) %all-to-all-start.4) | async-done | bytes 65568 | tf_op jit(solution)/shard_map/all_to_all | solution.py:162
  130.2 0.1 fusion.26
  130.3 0.2 fusion.13
  130.5 0.1 slice_add_fusion.2
  130.6 0.1 bitcast_multiply_fusion
  130.9 0.1 fusion.153
  131.0 0.2 fusion.107
  131.2 26.9 %all_to_all.30 = bf16[4,16,256]{2,1,0:T(8,128)(2,1)S(1)} all-to-all(bf16[4,16,256]{2,1,0:T(8,128)(2,1)S(1)} %broadcast_in_dim.76), channel_id=1, replica_groups=mesh['leaf'=128,'rank'=4] {'rank'}, dimensions={0} | all-to-all | bytes 65536 | tf_op jit(solution)/shard_map/all_to_all | solution.py:172
  158.1 0.3 convolution_bitcast_fusion
  158.4 0.6 fusion.31
  (90 shorter events, 2.5 us)
Async XLA Ops:
  0.0 0.8 copy-start
  1.1 8.0 %collective-permute-start = (f32[8,128]{1,0:T(8,128)S(1)}, f32[8,128]{1,0:T(8,128)S(1)}, u32[]{:S(2)}, u32[]{:S(2)}) collective-permute-start(f32[8,128]{1,0:T(8,128)S(1)} %pad_maximum_fusion.11), channel_id=1, source_target_pairs={{0,256},{4,260},{8,264},{12,268},{16,272},{20,276},{24,280},{28,28... | collective-permute-start | bytes 12296 | tf_op jit(solution)/shard_map/ppermute | solution.py:113
  7.7 1.0 copy-start.1
  8.3 30.9 %slice-start = ((bf16[8,4,2,64,256]{4,3,2,1,0:T(8,128)(2,1)}), bf16[1,4,2,64,256]{4,3,2,1,0:T(8,128)(2,1)S(1)}, s32[]{:S(2)}) async-start(bf16[8,4,2,64,256]{4,3,2,1,0:T(8,128)(2,1)} %param.7), calls=%async_computation.6 | async-start | bytes 524288 | tf_op jit(solution)/shard_map/slice | solution.py:152
  8.7 47.7 %slice-start.1 = ((bf16[8,4,2,64,256]{4,3,2,1,0:T(8,128)(2,1)}), bf16[1,4,2,64,256]{4,3,2,1,0:T(8,128)(2,1)S(1)}, s32[]{:S(2)}) async-start(bf16[8,4,2,64,256]{4,3,2,1,0:T(8,128)(2,1)} %param.7), calls=%async_computation.7 | async-start | bytes 524288 | tf_op jit(solution)/shard_map/slice | solution.py:152
  10.3 28.7 %all-to-all-start = ((f32[8,8,128]{2,1,0:T(8,128)}), f32[8,8,128]{2,1,0:T(8,128)S(1)}, u32[]{:S(2)}, u32[]{:S(2)}) async-start(f32[8,8,128]{2,1,0:T(8,128)} %bitcast.53), calls=%async_computation | async-start | bytes 65536 | tf_op jit(solution)/shard_map/all_to_all | solution.py:165
  40.2 15.9 %all-to-all-start.1 = ((f32[8,8,128]{2,1,0:T(8,128)}), f32[8,8,128]{2,1,0:T(8,128)S(1)}, u32[]{:S(2)}, u32[]{:S(2)}) async-start(f32[8,8,128]{2,1,0:T(8,128)} %bitcast.60), calls=%async_computation.1 | async-start | bytes 65536 | tf_op jit(solution)/shard_map/all_to_all | solution.py:165
  43.6 23.0 %collective-permute-start.1 = (bf16[4,4,64,128]{3,2,1,0:T(8,128)(2,1)S(1)}, bf16[4,4,64,128]{3,2,1,0:T(8,128)(2,1)S(1)}, u32[]{:S(2)}, u32[]{:S(2)}) collective-permute-start(bf16[4,4,64,128]{3,2,1,0:T(8,128)(2,1)S(1)} %pad_maximum_fusion.2), channel_id=1, source_target_pairs={{0,1},{1,0},{2,3},{3,2},{4,7},{5,6},{6,5},{7,4},{8,9},{9,8},{10,11... | collective-permute-start | bytes 786440 | tf_op jit(solution)/shard_map/ppermute | solution.py:123
  51.3 37.8 %slice-start.2 = ((bf16[8,4,2,64,256]{4,3,2,1,0:T(8,128)(2,1)}), bf16[1,4,2,64,256]{4,3,2,1,0:T(8,128)(2,1)S(1)}, s32[]{:S(2)}) async-start(bf16[8,4,2,64,256]{4,3,2,1,0:T(8,128)(2,1)} %param.7), calls=%async_computation.8 | async-start | bytes 524288 | tf_op jit(solution)/shard_map/slice | solution.py:152
  57.2 21.8 %all-to-all-start.2 = ((bf16[8,16,256]{2,1,0:T(8,128)(2,1)}), bf16[8,16,256]{2,1,0:T(8,128)(2,1)S(1)}, u32[]{:S(2)}, u32[]{:S(2)}) async-start(bf16[8,16,256]{2,1,0:T(8,128)(2,1)} %broadcast_in_dim.36), calls=%async_computation.2 | async-start | bytes 131072 | tf_op jit(solution)/shard_map/all_to_all | solution.py:162
  66.6 14.6 %collective-permute-start.3 = (bf16[2,4,64,128]{3,2,1,0:T(8,128)(2,1)S(1)}, bf16[2,4,64,128]{3,2,1,0:T(8,128)(2,1)S(1)}, u32[]{:S(2)}, u32[]{:S(2)}) collective-permute-start(bf16[2,4,64,128]{3,2,1,0:T(8,128)(2,1)S(1)} %pad_maximum_fusion.6), channel_id=1, source_target_pairs={{0,3},{1,2},{2,1},{3,0},{4,5},{5,4},{6,7},{7,6},{8,11},{9,10},{10,... | collective-permute-start | bytes 393224 | tf_op jit(solution)/shard_map/ppermute | solution.py:123
  81.3 31.7 %slice-start.3 = ((bf16[8,4,2,64,256]{4,3,2,1,0:T(8,128)(2,1)}), bf16[1,4,2,64,256]{4,3,2,1,0:T(8,128)(2,1)S(1)}, s32[]{:S(2)}) async-start(bf16[8,4,2,64,256]{4,3,2,1,0:T(8,128)(2,1)} %param.7), calls=%async_computation.9 | async-start | bytes 524288 | tf_op jit(solution)/shard_map/slice | solution.py:152
  81.9 7.0 %collective-permute-start.4 = (bf16[8,128]{1,0:T(8,128)(2,1)S(1)}, bf16[8,128]{1,0:T(8,128)(2,1)S(1)}, u32[]{:S(2)}, u32[]{:S(2)}) collective-permute-start(bf16[8,128]{1,0:T(8,128)(2,1)S(1)} %fusion.158), channel_id=1, source_target_pairs={{0,16},{4,20},{8,24},{12,28},{16,0},{20,4},{24,8},{28,12},{32,48},... | collective-permute-start | bytes 6152 | tf_op jit(solution)/shard_map/ppermute | solution.py:146
  90.1 22.6 %all-to-all-start.3 = ((f32[8,8,128]{2,1,0:T(8,128)}), f32[8,8,128]{2,1,0:T(8,128)S(1)}, u32[]{:S(2)}, u32[]{:S(2)}) async-start(f32[8,8,128]{2,1,0:T(8,128)} %bitcast.76), calls=%async_computation.3 | async-start | bytes 65536 | tf_op jit(solution)/shard_map/all_to_all | solution.py:165
  113.0 18.0 %slice-start.4 = ((bf16[8,4,2,64,256]{4,3,2,1,0:T(8,128)(2,1)}), bf16[1,4,2,64,256]{4,3,2,1,0:T(8,128)(2,1)S(1)}, s32[]{:S(2)}) async-start(bf16[8,4,2,64,256]{4,3,2,1,0:T(8,128)(2,1)} %param.7), calls=%async_computation.10 | async-start | bytes 524288 | tf_op jit(solution)/shard_map/slice | solution.py:152
  113.8 16.1 %all-to-all-start.4 = ((bf16[8,16,256]{2,1,0:T(8,128)(2,1)}), bf16[8,16,256]{2,1,0:T(8,128)(2,1)S(1)}, u32[]{:S(2)}, u32[]{:S(2)}) async-start(bf16[8,16,256]{2,1,0:T(8,128)(2,1)} %broadcast_in_dim.74), calls=%async_computation.4 | async-start | bytes 131072 | tf_op jit(solution)/shard_map/all_to_all | solution.py:162
  117.4 40.7 %copy-start.2 = (s32[4,256]{1,0:T(4,128)S(1)}, s32[4,256]{1,0:T(4,128)}, u32[]{:S(2)}) copy-start(s32[4,256]{1,0:T(4,128)} %param.5) | copy-start | bytes 12292
  117.4 12.6 %collective-permute-start.2 = (bf16[2,4,64,128]{3,2,1,0:T(8,128)(2,1)S(1)}, bf16[2,4,64,128]{3,2,1,0:T(8,128)(2,1)S(1)}, u32[]{:S(2)}, u32[]{:S(2)}) collective-permute-start(bf16[2,4,64,128]{3,2,1,0:T(8,128)(2,1)S(1)} %pad_maximum_fusion.5), channel_id=1, source_target_pairs={{0,3},{1,2},{2,1},{3,0},{4,5},{5,4},{6,7},{7,6},{8,11},{9,10},{10,... | collective-permute-start | bytes 393224 | tf_op jit(solution)/shard_map/ppermute | solution.py:123

commit v4 on v3

--- a/solution.py
+++ b/solution.py
@@ -91,11 +91,11 @@
     return jnp.stack([mine, after, far, before], axis=1).reshape(1024, 128)
 
 
-def column_product(own, partner, present, columns, rank):
-    partner = partner * jnp.repeat(present.astype(F32), 4)[:, None]
-    both = jnp.concatenate([own, partner], axis=0).astype(BF16)
-    turn = lax.dynamic_slice_in_dim(jnp.concatenate([both, both], axis=1), 64 * rank, 256, 1)
-    got = jnp.dot(per_block(jnp.concatenate([turn] * 4, axis=1)), columns, preferred_element_type=F32)
+def column_product(own, partner, present, columns, start, keep):
+    both = jnp.concatenate([own, partner * present], axis=0).astype(BF16)
+    turn = lax.dynamic_slice(jnp.concatenate([both, both], axis=1), (jnp.uint32(0), start), (32, 256))
+    wide = jnp.where(keep, jnp.concatenate([turn] * 4, axis=1), jnp.zeros((), BF16))
+    got = jnp.dot(wide, columns, preferred_element_type=F32)
     got = got[:16, :64] + got[16:, 64:]
     return jnp.concatenate([got[:8], got[8:]], axis=1)
 
@@ -138,10 +138,10 @@
             second, whole_own, whole_partner = lax.optimization_barrier((second, whole_own, whole_partner))
             columns[early] = assembled(of_early[0], first[0], second[0], second[1], first_is_next)
         elif level == late:
-            third, whole_own, whole_partner = lax.optimization_barrier((third, whole_own, whole_partner))
-            columns[late] = assembled(of_late[0], first[2], third[0], third[1], first_is_next)
+            fourth, whole_own, whole_partner = lax.optimization_barrier((fourth, whole_own, whole_partner))
+            columns[late] = assembled(of_late[0], third[0], fourth[0], fourth[1], first_is_next)
         if level in BY_COLUMNS:
-            own = column_product(whole_own, whole_partner, block_present[level], columns[level], rank)
+            own = column_product(whole_own, whole_partner, rows[level], columns[level], start, keep)
             if bit >= 0:
                 partner = lax.ppermute(own.astype(BF16), "leaf", [(at, at ^ 1 << bit) for at in range(leaves)])
                 partner = partner.astype(F32)
@@ -151,12 +151,21 @@
         part, factors = lax.optimization_barrier(
             (product(own, partner, tiles[level], factors[level].reshape(512, 256)), factors)
         )
+        if level == 1:
+            rows = [jnp.repeat(block_present[at].astype(F32), 4)[:, None] for at in BY_COLUMNS]
+            keep = jnp.arange(32)[:, None] // 4 % 4 == jnp.arange(1024)[None, :] // 256
+            part, first_is_next, start, keep, *rows = lax.optimization_barrier(
+                (part, first_is_next, (64 * rank).astype(jnp.uint32), keep, *rows)
+            )
+            rows = dict(zip(BY_COLUMNS, rows))
         if level == 0:
-            first = moved_on([of_early[1], of_early[3], of_late[1], of_late[3]], 0)
+            first = moved_on([of_early[1], of_early[3]], 0)
         elif level == 1:
             second = moved_on([of_early[2], first[1]], 1)
+        elif level == 2:
+            third = moved_on([of_late[1], of_late[3]], 0)
         elif level == 4:
-            third = moved_on([of_late[2], first[3]], 1)
+            fourth = moved_on([of_late[2], third[1]], 1)
         if level + 1 in BY_COLUMNS:
             sent = jnp.broadcast_to(part.astype(WIDE)[None], (2 * ranks, 16, 256))
             received = lax.all_to_all(sent, ("leaf", "rank"), 0, 0, axis_index_groups=groups, tiled=True)

time: 160 us -> 157 us (0.981)
  waiting for transfers between devices: 47.8 us -> 39.6 us
  starting transfers between devices: 70.7 us -> 76.3 us
    all_to_all x3, waiting for transfers between devices: 31.7 us -> 23.4 us  [local(): lax.all_to_all(chunks(part, 2), ('leaf', 'rank'), 0, 0, axis_index_groups...]
    ppermute x3 -> x4, starting transfers between devices: 23.3 us -> 31.4 us  [moved_on(): return lax.ppermute(jnp.stack(pieces), ('leaf', 'rank'), route)]
    all_to_all x2, starting transfers between devices: 12.3 us -> 9.83 us  [local(): lax.all_to_all(sent, ('leaf', 'rank'), 0, 0, axis_index_groups=groups, ti...]
  transfers between devices with their start and end apart: 10 -> 11, of which waited for: 7 -> 7; matrix products, arithmetic and copies ran while one was open for 3% -> 4% of each run, Pallas kernels for 0% -> 0%
where the time goes in v4:
time: 157 us; the launch traced here: 156 us
  starting transfers between devices  76.3 us (49%)
  waiting for transfers between devices  39.6 us (25%)
  blocking collectives  26.8 us (17%)
  local copies, waits for them, and re-layouts  6.98 us (4%)
  other arithmetic  4.09 us (3%)
  matrix products  1.99 us (1%)
    ppermute x4, starting transfers between devices, moved_on(): return lax.ppermute(jnp.stack(pieces), ('leaf', 'rank'), route)  31.4 us
    all_to_all x3, starting transfers between devices, local(): lax.all_to_all(chunks(part, 2), ('leaf', 'rank'), 0, 0, axis_index_groups...  27.6 us
    all_to_all x1, blocking collectives, local(): whole = lax.all_to_all(sent, 'rank', 0, 0, tiled=True).astype(F32).sum(0)  26.8 us
    all_to_all x3, waiting for transfers between devices, local(): lax.all_to_all(chunks(part, 2), ('leaf', 'rank'), 0, 0, axis_index_groups...  23.4 us
    all_to_all x2, waiting for transfers between devices, local(): lax.all_to_all(sent, ('leaf', 'rank'), 0, 0, axis_index_groups=groups, ti...  9.85 us
    all_to_all x2, starting transfers between devices, local(): lax.all_to_all(sent, ('leaf', 'rank'), 0, 0, axis_index_groups=groups, ti...  9.83 us
    ppermute x1, starting transfers between devices, local(): lax.ppermute(own, 'leaf', [(at, at ^ 1 << leaf_bits - 1) for at in range(...  5.1 us
    ppermute x1, waiting for transfers between devices, local(): lax.ppermute(own.astype(BF16), 'leaf', [(at, at ^ 1 << bit) for at in ran...  4.56 us
  transfers between devices with their start and end apart: 11, of which 7 were waited for; matrix products, arithmetic and copies ran while one was open for 4% of the time, Pallas kernels for 0%

profile of v4, /device:TPU:4, one launch (start us, length us, event | category | flops | bytes accessed | tf_op | source)
XLA Modules:
  0.0 156.3 jit_solution(10468278036578134763)
XLA Ops:
  0.0 0.8 constant_dynamic-slice_fusion
  0.8 0.2 convolution_bitcast_fusion.1
  1.1 5.1 %collective-permute-start = (f32[8,128]{1,0:T(8,128)S(1)}, f32[8,128]{1,0:T(8,128)S(1)}, u32[]{:S(2)}, u32[]{:S(2)}) collective-permute-start(f32[8,128]{1,0:T(8,128)S(1)} %pad_maximum_fusion.12), channel_id=1, source_target_pairs={{0,256},{4,260},{8,264},{12,268},{16,272},{20,276},{24,280},{28,28... | collective-permute-start | bytes 12296 | tf_op jit(solution)/shard_map/ppermute | solution.py:113
  6.3 1.2 slice_bitcast_fusion
  7.5 0.3 slice_bitcast_fusion.9
  7.7 0.1 maximum_bitcast_fusion.4
  7.8 0.1 maximum_bitcast_fusion.5
  7.9 0.1 maximum_bitcast_fusion.6
  8.0 0.1 maximum_bitcast_fusion.7
  8.1 0.1 maximum_bitcast_fusion
  8.2 0.1 maximum_bitcast_fusion.1
  8.4 0.1 maximum_bitcast_fusion.2
  8.5 0.1 maximum_bitcast_fusion.3
  8.8 0.1 copy.39
  8.9 0.1 broadcast_in_dim.32
  9.0 0.1 reshape.211
  9.2 0.1 fusion.129
  9.3 0.2 fusion.30
  9.6 0.1 fusion.131
  9.6 0.6 broadcast_in_dim.34
  10.3 15.2 %all-to-all-start = ((f32[8,8,128]{2,1,0:T(8,128)}), f32[8,8,128]{2,1,0:T(8,128)S(1)}, u32[]{:S(2)}, u32[]{:S(2)}) async-start(f32[8,8,128]{2,1,0:T(8,128)} %bitcast.47), calls=%async_computation | async-start | bytes 65536 | tf_op jit(solution)/shard_map/all_to_all | solution.py:174
  25.5 0.1 broadcast_compare_fusion
  25.6 0.2 convert_reduce_fusion.5
  25.9 0.1 broadcast_in_dim_reshape.6
  26.0 0.1 broadcast_in_dim_reshape.7
  26.1 12.8 %all-to-all-done = f32[8,8,128]{2,1,0:T(8,128)S(1)} async-done(((f32[8,8,128]{2,1,0:T(8,128)}), f32[8,8,128]{2,1,0:T(8,128)S(1)}, u32[]{:S(2)}, u32[]{:S(2)}) %all-to-all-start) | async-done | bytes 32800 | tf_op jit(solution)/shard_map/all_to_all | solution.py:174
  39.3 0.2 fusion.45
  39.5 0.1 fusion.137
  39.6 0.6 broadcast_in_dim.37
  40.2 3.3 %all-to-all-start.1 = ((f32[8,8,128]{2,1,0:T(8,128)}), f32[8,8,128]{2,1,0:T(8,128)S(1)}, u32[]{:S(2)}, u32[]{:S(2)}) async-start(f32[8,8,128]{2,1,0:T(8,128)} %bitcast.60), calls=%async_computation.1 | async-start | bytes 65536 | tf_op jit(solution)/shard_map/all_to_all | solution.py:174
  43.6 7.8 %collective-permute-start.3 = (bf16[2,4,64,128]{3,2,1,0:T(8,128)(2,1)S(1)}, bf16[2,4,64,128]{3,2,1,0:T(8,128)(2,1)S(1)}, u32[]{:S(2)}, u32[]{:S(2)}) collective-permute-start(bf16[2,4,64,128]{3,2,1,0:T(8,128)(2,1)S(1)} %pad_maximum_fusion.6), channel_id=1, source_target_pairs={{0,1},{1,0},{2,3},{3,2},{4,7},{5,6},{6,5},{7,4},{8,9},{9,8},{10,11... | collective-permute-start | bytes 393224 | tf_op jit(solution)/shard_map/ppermute | solution.py:123
  51.5 4.6 %all-to-all-done.1 = f32[8,8,128]{2,1,0:T(8,128)S(1)} async-done(((f32[8,8,128]{2,1,0:T(8,128)}), f32[8,8,128]{2,1,0:T(8,128)S(1)}, u32[]{:S(2)}, u32[]{:S(2)}) %all-to-all-start.1) | async-done | bytes 32800 | tf_op jit(solution)/shard_map/all_to_all | solution.py:174
  56.4 0.2 fusion.60
  56.6 0.6 broadcast_in_dim.38
  57.3 6.5 %all-to-all-start.2 = ((bf16[8,16,256]{2,1,0:T(8,128)(2,1)}), bf16[8,16,256]{2,1,0:T(8,128)(2,1)S(1)}, u32[]{:S(2)}, u32[]{:S(2)}) async-start(bf16[8,16,256]{2,1,0:T(8,128)(2,1)} %broadcast_in_dim.38), calls=%async_computation.2 | async-start | bytes 131072 | tf_op jit(solution)/shard_map/all_to_all | solution.py:171
  63.8 8.0 %collective-permute-start.4 = (bf16[2,4,64,128]{3,2,1,0:T(8,128)(2,1)S(1)}, bf16[2,4,64,128]{3,2,1,0:T(8,128)(2,1)S(1)}, u32[]{:S(2)}, u32[]{:S(2)}) collective-permute-start(bf16[2,4,64,128]{3,2,1,0:T(8,128)(2,1)S(1)} %pad_maximum_fusion.7), channel_id=1, source_target_pairs={{0,3},{1,2},{2,1},{3,0},{4,5},{5,4},{6,7},{7,6},{8,11},{9,10},{10,... | collective-permute-start | bytes 393224 | tf_op jit(solution)/shard_map/ppermute | solution.py:123
  71.8 4.9 %all-to-all-done.2 = bf16[8,16,256]{2,1,0:T(8,128)(2,1)S(1)} async-done(((bf16[8,16,256]{2,1,0:T(8,128)(2,1)}), bf16[8,16,256]{2,1,0:T(8,128)(2,1)S(1)}, u32[]{:S(2)}, u32[]{:S(2)}) %all-to-all-start.2) | async-done | bytes 65568 | tf_op jit(solution)/shard_map/all_to_all | solution.py:171
  76.8 1.8 %collective-permute-done.4 = bf16[2,4,64,128]{3,2,1,0:T(8,128)(2,1)S(1)} collective-permute-done((bf16[2,4,64,128]{3,2,1,0:T(8,128)(2,1)S(1)}, bf16[2,4,64,128]{3,2,1,0:T(8,128)(2,1)S(1)}, u32[]{:S(2)}, u32[]{:S(2)}) %collective-permute-start.4) | collective-permute-done | bytes 131104 | tf_op jit(solution)/shard_map/ppermute | solution.py:123
  78.7 0.1 fusion.27
  78.9 0.2 fusion.4
  79.0 0.1 slice_add_fusion.3
  79.2 2.4 %collective-permute-start.5 = (bf16[8,128]{1,0:T(8,128)(2,1)S(1)}, bf16[8,128]{1,0:T(8,128)(2,1)S(1)}, u32[]{:S(2)}, u32[]{:S(2)}) collective-permute-start(bf16[8,128]{1,0:T(8,128)(2,1)S(1)} %fusion.156), channel_id=1, source_target_pairs={{0,16},{4,20},{8,24},{12,28},{16,0},{20,4},{24,8},{28,12},{32,48},... | collective-permute-start | bytes 6152 | tf_op jit(solution)/shard_map/ppermute | solution.py:146
  81.6 4.6 %collective-permute-done.5 = bf16[8,128]{1,0:T(8,128)(2,1)S(1)} collective-permute-done((bf16[8,128]{1,0:T(8,128)(2,1)S(1)}, bf16[8,128]{1,0:T(8,128)(2,1)S(1)}, u32[]{:S(2)}, u32[]{:S(2)}) %collective-permute-start.5) | collective-permute-done | bytes 2080 | tf_op jit(solution)/shard_map/ppermute | solution.py:146
  86.3 0.1 fusion.143
  86.4 0.2 fusion.75
  86.7 0.1 fusion.145
  86.8 0.6 broadcast_in_dim.76
  87.4 9.1 %all-to-all-start.3 = ((f32[8,8,128]{2,1,0:T(8,128)}), f32[8,8,128]{2,1,0:T(8,128)S(1)}, u32[]{:S(2)}, u32[]{:S(2)}) async-start(f32[8,8,128]{2,1,0:T(8,128)} %bitcast.77), calls=%async_computation.3 | async-start | bytes 65536 | tf_op jit(solution)/shard_map/all_to_all | solution.py:174
  96.5 7.8 %collective-permute-start.1 = (bf16[2,4,64,128]{3,2,1,0:T(8,128)(2,1)S(1)}, bf16[2,4,64,128]{3,2,1,0:T(8,128)(2,1)S(1)}, u32[]{:S(2)}, u32[]{:S(2)}) collective-permute-start(bf16[2,4,64,128]{3,2,1,0:T(8,128)(2,1)S(1)} %pad_maximum_fusion.4), channel_id=1, source_target_pairs={{0,1},{1,0},{2,3},{3,2},{4,7},{5,6},{6,5},{7,4},{8,9},{9,8},{10,11... | collective-permute-start | bytes 393224 | tf_op jit(solution)/shard_map/ppermute | solution.py:123
  104.3 5.9 %all-to-all-done.3 = f32[8,8,128]{2,1,0:T(8,128)S(1)} async-done(((f32[8,8,128]{2,1,0:T(8,128)}), f32[8,8,128]{2,1,0:T(8,128)S(1)}, u32[]{:S(2)}, u32[]{:S(2)}) %all-to-all-start.3) | async-done | bytes 32800 | tf_op jit(solution)/shard_map/all_to_all | solution.py:174
  110.5 0.2 fusion.90
  110.7 0.6 broadcast_in_dim.77
  111.4 3.3 %all-to-all-start.4 = ((bf16[8,16,256]{2,1,0:T(8,128)(2,1)}), bf16[8,16,256]{2,1,0:T(8,128)(2,1)S(1)}, u32[]{:S(2)}, u32[]{:S(2)}) async-start(bf16[8,16,256]{2,1,0:T(8,128)(2,1)} %broadcast_in_dim.77), calls=%async_computation.4 | async-start | bytes 131072 | tf_op jit(solution)/shard_map/all_to_all | solution.py:171
  114.8 7.7 %collective-permute-start.2 = (bf16[2,4,64,128]{3,2,1,0:T(8,128)(2,1)S(1)}, bf16[2,4,64,128]{3,2,1,0:T(8,128)(2,1)S(1)}, u32[]{:S(2)}, u32[]{:S(2)}) collective-permute-start(bf16[2,4,64,128]{3,2,1,0:T(8,128)(2,1)S(1)} %pad_maximum_fusion.5), channel_id=1, source_target_pairs={{0,3},{1,2},{2,1},{3,0},{4,5},{5,4},{6,7},{7,6},{8,11},{9,10},{10,... | collective-permute-start | bytes 393224 | tf_op jit(solution)/shard_map/ppermute | solution.py:123
  122.5 4.9 %all-to-all-done.4 = bf16[8,16,256]{2,1,0:T(8,128)(2,1)S(1)} async-done(((bf16[8,16,256]{2,1,0:T(8,128)(2,1)}), bf16[8,16,256]{2,1,0:T(8,128)(2,1)S(1)}, u32[]{:S(2)}, u32[]{:S(2)}) %all-to-all-start.4) | async-done | bytes 65568 | tf_op jit(solution)/shard_map/all_to_all | solution.py:171
  127.6 0.1 fusion.24
  127.8 0.2 fusion.11
  127.9 0.1 slice_add_fusion.2
  128.0 0.1 bitcast_multiply_fusion
  128.3 0.1 fusion.151
  128.3 0.2 fusion.105
  128.5 26.8 %all_to_all.30 = bf16[4,16,256]{2,1,0:T(8,128)(2,1)S(1)} all-to-all(bf16[4,16,256]{2,1,0:T(8,128)(2,1)S(1)} %broadcast_in_dim.78), channel_id=1, replica_groups=mesh['leaf'=128,'rank'=4] {'rank'}, dimensions={0} | all-to-all | bytes 65536 | tf_op jit(solution)/shard_map/all_to_all | solution.py:181
  155.4 0.3 convolution_bitcast_fusion
  155.7 0.6 fusion.29
  (93 shorter events, 2.6 us)
Async XLA Ops:
  0.0 0.8 copy-start
  1.1 8.0 %collective-permute-start = (f32[8,128]{1,0:T(8,128)S(1)}, f32[8,128]{1,0:T(8,128)S(1)}, u32[]{:S(2)}, u32[]{:S(2)}) collective-permute-start(f32[8,128]{1,0:T(8,128)S(1)} %pad_maximum_fusion.12), channel_id=1, source_target_pairs={{0,256},{4,260},{8,264},{12,268},{16,272},{20,276},{24,280},{28,28... | collective-permute-start | bytes 12296 | tf_op jit(solution)/shard_map/ppermute | solution.py:113
  7.7 1.0 copy-start.1
  8.3 30.9 %slice-start = ((bf16[8,4,2,64,256]{4,3,2,1,0:T(8,128)(2,1)}), bf16[1,4,2,64,256]{4,3,2,1,0:T(8,128)(2,1)S(1)}, s32[]{:S(2)}) async-start(bf16[8,4,2,64,256]{4,3,2,1,0:T(8,128)(2,1)} %param.7), calls=%async_computation.6 | async-start | bytes 524288 | tf_op jit(solution)/shard_map/slice | solution.py:152
  8.7 47.8 %slice-start.1 = ((bf16[8,4,2,64,256]{4,3,2,1,0:T(8,128)(2,1)}), bf16[1,4,2,64,256]{4,3,2,1,0:T(8,128)(2,1)S(1)}, s32[]{:S(2)}) async-start(bf16[8,4,2,64,256]{4,3,2,1,0:T(8,128)(2,1)} %param.7), calls=%async_computation.7 | async-start | bytes 524288 | tf_op jit(solution)/shard_map/slice | solution.py:152
  10.3 28.7 %all-to-all-start = ((f32[8,8,128]{2,1,0:T(8,128)}), f32[8,8,128]{2,1,0:T(8,128)S(1)}, u32[]{:S(2)}, u32[]{:S(2)}) async-start(f32[8,8,128]{2,1,0:T(8,128)} %bitcast.47), calls=%async_computation | async-start | bytes 65536 | tf_op jit(solution)/shard_map/all_to_all | solution.py:174
  40.2 15.9 %all-to-all-start.1 = ((f32[8,8,128]{2,1,0:T(8,128)}), f32[8,8,128]{2,1,0:T(8,128)S(1)}, u32[]{:S(2)}, u32[]{:S(2)}) async-start(f32[8,8,128]{2,1,0:T(8,128)} %bitcast.60), calls=%async_computation.1 | async-start | bytes 65536 | tf_op jit(solution)/shard_map/all_to_all | solution.py:174
  43.6 42.8 %slice-start.2 = ((bf16[8,4,2,64,256]{4,3,2,1,0:T(8,128)(2,1)}), bf16[1,4,2,64,256]{4,3,2,1,0:T(8,128)(2,1)S(1)}, s32[]{:S(2)}) async-start(bf16[8,4,2,64,256]{4,3,2,1,0:T(8,128)(2,1)} %param.7), calls=%async_computation.8 | async-start | bytes 524288 | tf_op jit(solution)/shard_map/slice | solution.py:152
  43.6 20.1 %collective-permute-start.3 = (bf16[2,4,64,128]{3,2,1,0:T(8,128)(2,1)S(1)}, bf16[2,4,64,128]{3,2,1,0:T(8,128)(2,1)S(1)}, u32[]{:S(2)}, u32[]{:S(2)}) collective-permute-start(bf16[2,4,64,128]{3,2,1,0:T(8,128)(2,1)S(1)} %pad_maximum_fusion.6), channel_id=1, source_target_pairs={{0,1},{1,0},{2,3},{3,2},{4,7},{5,6},{6,5},{7,4},{8,9},{9,8},{10,11... | collective-permute-start | bytes 393224 | tf_op jit(solution)/shard_map/ppermute | solution.py:123
  57.3 19.5 %all-to-all-start.2 = ((bf16[8,16,256]{2,1,0:T(8,128)(2,1)}), bf16[8,16,256]{2,1,0:T(8,128)(2,1)S(1)}, u32[]{:S(2)}, u32[]{:S(2)}) async-start(bf16[8,16,256]{2,1,0:T(8,128)(2,1)} %broadcast_in_dim.38), calls=%async_computation.2 | async-start | bytes 131072 | tf_op jit(solution)/shard_map/all_to_all | solution.py:171
  63.8 46.7 %slice-start.3 = ((bf16[8,4,2,64,256]{4,3,2,1,0:T(8,128)(2,1)}), bf16[1,4,2,64,256]{4,3,2,1,0:T(8,128)(2,1)S(1)}, s32[]{:S(2)}) async-start(bf16[8,4,2,64,256]{4,3,2,1,0:T(8,128)(2,1)} %param.7), calls=%async_computation.9 | async-start | bytes 524288 | tf_op jit(solution)/shard_map/slice | solution.py:152
  63.8 14.8 %collective-permute-start.4 = (bf16[2,4,64,128]{3,2,1,0:T(8,128)(2,1)S(1)}, bf16[2,4,64,128]{3,2,1,0:T(8,128)(2,1)S(1)}, u32[]{:S(2)}, u32[]{:S(2)}) collective-permute-start(bf16[2,4,64,128]{3,2,1,0:T(8,128)(2,1)S(1)} %pad_maximum_fusion.7), channel_id=1, source_target_pairs={{0,3},{1,2},{2,1},{3,0},{4,5},{5,4},{6,7},{7,6},{8,11},{9,10},{10,... | collective-permute-start | bytes 393224 | tf_op jit(solution)/shard_map/ppermute | solution.py:123
  79.2 7.0 %collective-permute-start.5 = (bf16[8,128]{1,0:T(8,128)(2,1)S(1)}, bf16[8,128]{1,0:T(8,128)(2,1)S(1)}, u32[]{:S(2)}, u32[]{:S(2)}) collective-permute-start(bf16[8,128]{1,0:T(8,128)(2,1)S(1)} %fusion.156), channel_id=1, source_target_pairs={{0,16},{4,20},{8,24},{12,28},{16,0},{20,4},{24,8},{28,12},{32,48},... | collective-permute-start | bytes 6152 | tf_op jit(solution)/shard_map/ppermute | solution.py:146
  87.4 22.8 %all-to-all-start.3 = ((f32[8,8,128]{2,1,0:T(8,128)}), f32[8,8,128]{2,1,0:T(8,128)S(1)}, u32[]{:S(2)}, u32[]{:S(2)}) async-start(f32[8,8,128]{2,1,0:T(8,128)} %bitcast.77), calls=%async_computation.3 | async-start | bytes 65536 | tf_op jit(solution)/shard_map/all_to_all | solution.py:174
  96.5 18.3 %collective-permute-start.1 = (bf16[2,4,64,128]{3,2,1,0:T(8,128)(2,1)S(1)}, bf16[2,4,64,128]{3,2,1,0:T(8,128)(2,1)S(1)}, u32[]{:S(2)}, u32[]{:S(2)}) collective-permute-start(bf16[2,4,64,128]{3,2,1,0:T(8,128)(2,1)S(1)} %pad_maximum_fusion.4), channel_id=1, source_target_pairs={{0,1},{1,0},{2,3},{3,2},{4,7},{5,6},{6,5},{7,4},{8,9},{9,8},{10,11... | collective-permute-start | bytes 393224 | tf_op jit(solution)/shard_map/ppermute | solution.py:123
  104.3 24.0 %slice-start.4 = ((bf16[8,4,2,64,256]{4,3,2,1,0:T(8,128)(2,1)}), bf16[1,4,2,64,256]{4,3,2,1,0:T(8,128)(2,1)S(1)}, s32[]{:S(2)}) async-start(bf16[8,4,2,64,256]{4,3,2,1,0:T(8,128)(2,1)} %param.7), calls=%async_computation.10 | async-start | bytes 524288 | tf_op jit(solution)/shard_map/slice | solution.py:152
  110.7 44.7 %copy-start.2 = (s32[4,256]{1,0:T(4,128)S(1)}, s32[4,256]{1,0:T(4,128)}, u32[]{:S(2)}) copy-start(s32[4,256]{1,0:T(4,128)} %param.5) | copy-start | bytes 12292
  111.4 16.1 %all-to-all-start.4 = ((bf16[8,16,256]{2,1,0:T(8,128)(2,1)}), bf16[8,16,256]{2,1,0:T(8,128)(2,1)S(1)}, u32[]{:S(2)}, u32[]{:S(2)}) async-start(bf16[8,16,256]{2,1,0:T(8,128)(2,1)} %broadcast_in_dim.77), calls=%async_computation.4 | async-start | bytes 131072 | tf_op jit(solution)/shard_map/all_to_all | solution.py:171
  114.8 12.7 %collective-permute-start.2 = (bf16[2,4,64,128]{3,2,1,0:T(8,128)(2,1)S(1)}, bf16[2,4,64,128]{3,2,1,0:T(8,128)(2,1)S(1)}, u32[]{:S(2)}, u32[]{:S(2)}) collective-permute-start(bf16[2,4,64,128]{3,2,1,0:T(8,128)(2,1)S(1)} %pad_maximum_fusion.5), channel_id=1, source_target_pairs={{0,3},{1,2},{2,1},{3,0},{4,5},{5,4},{6,7},{7,6},{8,11},{9,10},{10,... | collective-permute-start | bytes 393224 | tf_op jit(solution)/shard_map/ppermute | solution.py:123

commit v5 on v4

--- a/solution.py
+++ b/solution.py
@@ -134,12 +134,6 @@
     for level in range(LEVELS):
         bit = leaf_bits - 2 - level
         groups = pair_groups(leaves, ranks, bit) if bit >= 0 else None
-        if level == early:
-            second, whole_own, whole_partner = lax.optimization_barrier((second, whole_own, whole_partner))
-            columns[early] = assembled(of_early[0], first[0], second[0], second[1], first_is_next)
-        elif level == late:
-            fourth, whole_own, whole_partner = lax.optimization_barrier((fourth, whole_own, whole_partner))
-            columns[late] = assembled(of_late[0], third[0], fourth[0], fourth[1], first_is_next)
         if level in BY_COLUMNS:
             own = column_product(whole_own, whole_partner, rows[level], columns[level], start, keep)
             if bit >= 0:
@@ -166,6 +160,12 @@
             third = moved_on([of_late[1], of_late[3]], 0)
         elif level == 4:
             fourth = moved_on([of_late[2], third[1]], 1)
+        if level + 1 == early:
+            part, mine, near = lax.optimization_barrier((part, of_early[0], first[0]))
+            columns[early] = assembled(mine, near, second[0], second[1], first_is_next)
+        elif level + 1 == late:
+            part, mine, near = lax.optimization_barrier((part, of_late[0], third[0]))
+            columns[late] = assembled(mine, near, fourth[0], fourth[1], first_is_next)
         if level + 1 in BY_COLUMNS:
             sent = jnp.broadcast_to(part.astype(WIDE)[None], (2 * ranks, 16, 256))
             received = lax.all_to_all(sent, ("leaf", "rank"), 0, 0, axis_index_groups=groups, tiled=True)

time: 157 us -> 150 us (0.955)
  the two profiles are of different devices: /device:TPU:4 before, /device:TPU:1 now
where the time goes in v5:
time: 150 us; the launch traced here: 149 us
  starting transfers between devices  75.6 us (50%)
  waiting for transfers between devices  44.5 us (30%)
  blocking collectives  15.4 us (10%)
  local copies, waits for them, and re-layouts  6.99 us (5%)
  other arithmetic  4.08 us (3%)
  matrix products  1.99 us (1%)
    ppermute x4, starting transfers between devices, moved_on(): return lax.ppermute(jnp.stack(pieces), ('leaf', 'rank'), route)  29.7 us
    all_to_all x2, waiting for transfers between devices, local(): lax.all_to_all(sent, ('leaf', 'rank'), 0, 0, axis_index_groups=groups, ti...  23.6 us
    all_to_all x2, starting transfers between devices, local(): lax.all_to_all(sent, ('leaf', 'rank'), 0, 0, axis_index_groups=groups, ti...  20.8 us
    all_to_all x3, waiting for transfers between devices, local(): lax.all_to_all(chunks(part, 2), ('leaf', 'rank'), 0, 0, axis_index_groups...  17.6 us
    all_to_all x1, blocking collectives, local(): whole = lax.all_to_all(sent, 'rank', 0, 0, tiled=True).astype(F32).sum(0)  15.4 us
    all_to_all x3, starting transfers between devices, local(): lax.all_to_all(chunks(part, 2), ('leaf', 'rank'), 0, 0, axis_index_groups...  14.9 us
    ppermute x1, starting transfers between devices, local(): lax.ppermute(own, 'leaf', [(at, at ^ 1 << leaf_bits - 1) for at in range(...  5.64 us
    ppermute x1, starting transfers between devices, local(): lax.ppermute(own.astype(BF16), 'leaf', [(at, at ^ 1 << bit) for at in ran...  4.65 us
  transfers between devices with their start and end apart: 11, of which 6 were waited for; matrix products, arithmetic and copies ran while one was open for 6% of the time, Pallas kernels for 0%

profile of v5, /device:TPU:1, one launch (start us, length us, event | category | flops | bytes accessed | tf_op | source)
XLA Modules:
  0.0 149.1 jit_solution(9860972043801104662)
XLA Ops:
  0.0 0.8 constant_dynamic-slice_fusion
  0.8 0.2 convolution_bitcast_fusion.1
  1.1 5.6 %collective-permute-start = (f32[8,128]{1,0:T(8,128)S(1)}, f32[8,128]{1,0:T(8,128)S(1)}, u32[]{:S(2)}, u32[]{:S(2)}) collective-permute-start(f32[8,128]{1,0:T(8,128)S(1)} %pad_maximum_fusion.12), channel_id=1, source_target_pairs={{0,256},{4,260},{8,264},{12,268},{16,272},{20,276},{24,280},{28,28... | collective-permute-start | bytes 12296 | tf_op jit(solution)/shard_map/ppermute | solution.py:113
  6.8 1.2 slice_bitcast_fusion
  8.0 0.3 slice_bitcast_fusion.15
  8.3 0.1 maximum_bitcast_fusion.4
  8.4 0.1 maximum_bitcast_fusion.5
  8.5 0.1 maximum_bitcast_fusion.6
  8.6 0.1 maximum_bitcast_fusion.7
  8.7 0.1 maximum_bitcast_fusion
  8.8 0.1 maximum_bitcast_fusion.1
  8.9 0.1 maximum_bitcast_fusion.2
  9.0 0.1 maximum_bitcast_fusion.3
  9.2 0.1 broadcast_compare_fusion
  9.4 0.1 copy.39
  9.5 0.1 broadcast_in_dim.32
  9.6 0.1 reshape.135
  9.7 12.6 %collective-permute-start.4 = (bf16[2,4,64,128]{3,2,1,0:T(8,128)(2,1)S(1)}, bf16[2,4,64,128]{3,2,1,0:T(8,128)(2,1)S(1)}, u32[]{:S(2)}, u32[]{:S(2)}) collective-permute-start(bf16[2,4,64,128]{3,2,1,0:T(8,128)(2,1)S(1)} %pad_maximum_fusion.6), channel_id=1, source_target_pairs={{0,1},{1,0},{2,3},{3,2},{4,7},{5,6},{6,5},{7,4},{8,9},{9,8},{10,11... | collective-permute-start | bytes 393224 | tf_op jit(solution)/shard_map/ppermute | solution.py:123
  22.5 0.1 fusion.129
  22.5 0.2 fusion.30
  22.8 0.1 fusion.131
  22.9 0.6 broadcast_in_dim.34
  23.5 4.7 %all-to-all-start = ((f32[8,8,128]{2,1,0:T(8,128)}), f32[8,8,128]{2,1,0:T(8,128)S(1)}, u32[]{:S(2)}, u32[]{:S(2)}) async-start(f32[8,8,128]{2,1,0:T(8,128)} %bitcast.47), calls=%async_computation | async-start | bytes 65536 | tf_op jit(solution)/shard_map/all_to_all | solution.py:174
  28.2 7.3 %collective-permute-start.1 = (bf16[2,4,64,128]{3,2,1,0:T(8,128)(2,1)S(1)}, bf16[2,4,64,128]{3,2,1,0:T(8,128)(2,1)S(1)}, u32[]{:S(2)}, u32[]{:S(2)}) collective-permute-start(bf16[2,4,64,128]{3,2,1,0:T(8,128)(2,1)S(1)} %pad_maximum_fusion.4), channel_id=1, source_target_pairs={{0,1},{1,0},{2,3},{3,2},{4,7},{5,6},{6,5},{7,4},{8,9},{9,8},{10,11... | collective-permute-start | bytes 393224 | tf_op jit(solution)/shard_map/ppermute | solution.py:123
  35.5 0.2 convert_reduce_fusion.5
  35.8 0.1 broadcast_in_dim_reshape.6
  35.9 0.1 broadcast_in_dim_reshape.7
  36.0 4.5 %all-to-all-done = f32[8,8,128]{2,1,0:T(8,128)S(1)} async-done(((f32[8,8,128]{2,1,0:T(8,128)}), f32[8,8,128]{2,1,0:T(8,128)S(1)}, u32[]{:S(2)}, u32[]{:S(2)}) %all-to-all-start) | async-done | bytes 32800 | tf_op jit(solution)/shard_map/all_to_all | solution.py:174
  40.8 0.2 fusion.45
  41.1 0.1 fusion.137
  41.2 0.6 broadcast_in_dim.37
  41.8 3.3 %all-to-all-start.1 = ((f32[8,8,128]{2,1,0:T(8,128)}), f32[8,8,128]{2,1,0:T(8,128)S(1)}, u32[]{:S(2)}, u32[]{:S(2)}) async-start(f32[8,8,128]{2,1,0:T(8,128)} %bitcast.54), calls=%async_computation.1 | async-start | bytes 65536 | tf_op jit(solution)/shard_map/all_to_all | solution.py:174
  45.2 7.3 %collective-permute-start.2 = (bf16[2,4,64,128]{3,2,1,0:T(8,128)(2,1)S(1)}, bf16[2,4,64,128]{3,2,1,0:T(8,128)(2,1)S(1)}, u32[]{:S(2)}, u32[]{:S(2)}) collective-permute-start(bf16[2,4,64,128]{3,2,1,0:T(8,128)(2,1)S(1)} %pad_maximum_fusion.5), channel_id=1, source_target_pairs={{0,3},{1,2},{2,1},{3,0},{4,5},{5,4},{6,7},{7,6},{8,11},{9,10},{10,... | collective-permute-start | bytes 393224 | tf_op jit(solution)/shard_map/ppermute | solution.py:123
  52.5 4.1 %all-to-all-done.1 = f32[8,8,128]{2,1,0:T(8,128)S(1)} async-done(((f32[8,8,128]{2,1,0:T(8,128)}), f32[8,8,128]{2,1,0:T(8,128)S(1)}, u32[]{:S(2)}, u32[]{:S(2)}) %all-to-all-start.1) | async-done | bytes 32800 | tf_op jit(solution)/shard_map/all_to_all | solution.py:174
  56.9 0.2 fusion.60
  57.1 0.6 broadcast_in_dim.38
  57.8 3.3 %all-to-all-start.2 = ((bf16[8,16,256]{2,1,0:T(8,128)(2,1)}), bf16[8,16,256]{2,1,0:T(8,128)(2,1)S(1)}, u32[]{:S(2)}, u32[]{:S(2)}) async-start(bf16[8,16,256]{2,1,0:T(8,128)(2,1)} %broadcast_in_dim.38), calls=%async_computation.2 | async-start | bytes 131072 | tf_op jit(solution)/shard_map/all_to_all | solution.py:171
  61.2 11.3 %all-to-all-done.2 = bf16[8,16,256]{2,1,0:T(8,128)(2,1)S(1)} async-done(((bf16[8,16,256]{2,1,0:T(8,128)(2,1)}), bf16[8,16,256]{2,1,0:T(8,128)(2,1)S(1)}, u32[]{:S(2)}, u32[]{:S(2)}) %all-to-all-start.2) | async-done | bytes 65568 | tf_op jit(solution)/shard_map/all_to_all | solution.py:171
  72.6 0.1 fusion.27
  72.7 0.2 fusion.4
  72.9 0.1 slice_add_fusion.3
  73.0 4.7 %collective-permute-start.3 = (bf16[8,128]{1,0:T(8,128)(2,1)S(1)}, bf16[8,128]{1,0:T(8,128)(2,1)S(1)}, u32[]{:S(2)}, u32[]{:S(2)}) collective-permute-start(bf16[8,128]{1,0:T(8,128)(2,1)S(1)} %fusion.156), channel_id=1, source_target_pairs={{0,16},{4,20},{8,24},{12,28},{16,0},{20,4},{24,8},{28,12},{32,48},... | collective-permute-start | bytes 6152 | tf_op jit(solution)/shard_map/ppermute | solution.py:140
  77.7 2.5 %collective-permute-start.5 = (bf16[2,4,64,128]{3,2,1,0:T(8,128)(2,1)S(1)}, bf16[2,4,64,128]{3,2,1,0:T(8,128)(2,1)S(1)}, u32[]{:S(2)}, u32[]{:S(2)}) collective-permute-start(bf16[2,4,64,128]{3,2,1,0:T(8,128)(2,1)S(1)} %pad_maximum_fusion.7), channel_id=1, source_target_pairs={{0,3},{1,2},{2,1},{3,0},{4,5},{5,4},{6,7},{7,6},{8,11},{9,10},{10,... | collective-permute-start | bytes 393224 | tf_op jit(solution)/shard_map/ppermute | solution.py:123
  80.4 0.1 fusion.143
  80.5 0.2 fusion.75
  80.8 0.1 fusion.145
  80.9 0.6 broadcast_in_dim.76
  81.5 6.9 %all-to-all-start.3 = ((f32[8,8,128]{2,1,0:T(8,128)}), f32[8,8,128]{2,1,0:T(8,128)S(1)}, u32[]{:S(2)}, u32[]{:S(2)}) async-start(f32[8,8,128]{2,1,0:T(8,128)} %bitcast.76), calls=%async_computation.3 | async-start | bytes 65536 | tf_op jit(solution)/shard_map/all_to_all | solution.py:174
  88.4 3.3 %collective-permute-done.5 = bf16[2,4,64,128]{3,2,1,0:T(8,128)(2,1)S(1)} collective-permute-done((bf16[2,4,64,128]{3,2,1,0:T(8,128)(2,1)S(1)}, bf16[2,4,64,128]{3,2,1,0:T(8,128)(2,1)S(1)}, u32[]{:S(2)}, u32[]{:S(2)}) %collective-permute-start.5) | collective-permute-done | bytes 131104 | tf_op jit(solution)/shard_map/ppermute | solution.py:123
  91.7 9.0 %all-to-all-done.3 = f32[8,8,128]{2,1,0:T(8,128)S(1)} async-done(((f32[8,8,128]{2,1,0:T(8,128)}), f32[8,8,128]{2,1,0:T(8,128)S(1)}, u32[]{:S(2)}, u32[]{:S(2)}) %all-to-all-start.3) | async-done | bytes 32800 | tf_op jit(solution)/shard_map/all_to_all | solution.py:174
  101.0 0.2 fusion.90
  101.2 0.6 broadcast_in_dim.77
  101.9 17.4 %all-to-all-start.4 = ((bf16[8,16,256]{2,1,0:T(8,128)(2,1)}), bf16[8,16,256]{2,1,0:T(8,128)(2,1)S(1)}, u32[]{:S(2)}, u32[]{:S(2)}) async-start(bf16[8,16,256]{2,1,0:T(8,128)(2,1)} %broadcast_in_dim.77), calls=%async_computation.4 | async-start | bytes 131072 | tf_op jit(solution)/shard_map/all_to_all | solution.py:171
  119.4 12.3 %all-to-all-done.4 = bf16[8,16,256]{2,1,0:T(8,128)(2,1)S(1)} async-done(((bf16[8,16,256]{2,1,0:T(8,128)(2,1)}), bf16[8,16,256]{2,1,0:T(8,128)(2,1)S(1)}, u32[]{:S(2)}, u32[]{:S(2)}) %all-to-all-start.4) | async-done | bytes 65568 | tf_op jit(solution)/shard_map/all_to_all | solution.py:171
  131.7 0.1 multiply_convert_fusion
  131.8 0.1 fusion.24
  131.9 0.2 fusion.11
  132.1 0.1 slice_add_fusion.2
  132.2 0.1 bitcast_multiply_fusion
  132.4 0.1 fusion.151
  132.5 0.2 fusion.105
  132.7 15.4 %all_to_all.30 = bf16[4,16,256]{2,1,0:T(8,128)(2,1)S(1)} all-to-all(bf16[4,16,256]{2,1,0:T(8,128)(2,1)S(1)} %broadcast_in_dim.78), channel_id=1, replica_groups=mesh['leaf'=128,'rank'=4] {'rank'}, dimensions={0} | all-to-all | bytes 65536 | tf_op jit(solution)/shard_map/all_to_all | solution.py:181
  148.2 0.3 convolution_bitcast_fusion
  148.4 0.6 fusion.29
  (93 shorter events, 2.6 us)
Async XLA Ops:
  0.0 0.8 copy-start
  1.1 8.6 %collective-permute-start = (f32[8,128]{1,0:T(8,128)S(1)}, f32[8,128]{1,0:T(8,128)S(1)}, u32[]{:S(2)}, u32[]{:S(2)}) collective-permute-start(f32[8,128]{1,0:T(8,128)S(1)} %pad_maximum_fusion.12), channel_id=1, source_target_pairs={{0,256},{4,260},{8,264},{12,268},{16,272},{20,276},{24,280},{28,28... | collective-permute-start | bytes 12296 | tf_op jit(solution)/shard_map/ppermute | solution.py:113
  8.3 1.1 copy-start.1
  9.1 31.8 %slice-start = ((bf16[8,4,2,64,256]{4,3,2,1,0:T(8,128)(2,1)}), bf16[1,4,2,64,256]{4,3,2,1,0:T(8,128)(2,1)S(1)}, s32[]{:S(2)}) async-start(bf16[8,4,2,64,256]{4,3,2,1,0:T(8,128)(2,1)} %param.7), calls=%async_computation.6 | async-start | bytes 524288 | tf_op jit(solution)/shard_map/slice | solution.py:146
  9.7 47.3 %slice-start.1 = ((bf16[8,4,2,64,256]{4,3,2,1,0:T(8,128)(2,1)}), bf16[1,4,2,64,256]{4,3,2,1,0:T(8,128)(2,1)S(1)}, s32[]{:S(2)}) async-start(bf16[8,4,2,64,256]{4,3,2,1,0:T(8,128)(2,1)} %param.7), calls=%async_computation.7 | async-start | bytes 524288 | tf_op jit(solution)/shard_map/slice | solution.py:146
  9.7 42.8 %collective-permute-start.4 = (bf16[2,4,64,128]{3,2,1,0:T(8,128)(2,1)S(1)}, bf16[2,4,64,128]{3,2,1,0:T(8,128)(2,1)S(1)}, u32[]{:S(2)}, u32[]{:S(2)}) collective-permute-start(bf16[2,4,64,128]{3,2,1,0:T(8,128)(2,1)S(1)} %pad_maximum_fusion.6), channel_id=1, source_target_pairs={{0,1},{1,0},{2,3},{3,2},{4,7},{5,6},{6,5},{7,4},{8,9},{9,8},{10,11... | collective-permute-start | bytes 393224 | tf_op jit(solution)/shard_map/ppermute | solution.py:123
  23.5 17.0 %all-to-all-start = ((f32[8,8,128]{2,1,0:T(8,128)}), f32[8,8,128]{2,1,0:T(8,128)S(1)}, u32[]{:S(2)}, u32[]{:S(2)}) async-start(f32[8,8,128]{2,1,0:T(8,128)} %bitcast.47), calls=%async_computation | async-start | bytes 65536 | tf_op jit(solution)/shard_map/all_to_all | solution.py:174
  28.2 17.0 %collective-permute-start.1 = (bf16[2,4,64,128]{3,2,1,0:T(8,128)(2,1)S(1)}, bf16[2,4,64,128]{3,2,1,0:T(8,128)(2,1)S(1)}, u32[]{:S(2)}, u32[]{:S(2)}) collective-permute-start(bf16[2,4,64,128]{3,2,1,0:T(8,128)(2,1)S(1)} %pad_maximum_fusion.4), channel_id=1, source_target_pairs={{0,1},{1,0},{2,3},{3,2},{4,7},{5,6},{6,5},{7,4},{8,9},{9,8},{10,11... | collective-permute-start | bytes 393224 | tf_op jit(solution)/shard_map/ppermute | solution.py:123
  41.8 14.8 %all-to-all-start.1 = ((f32[8,8,128]{2,1,0:T(8,128)}), f32[8,8,128]{2,1,0:T(8,128)S(1)}, u32[]{:S(2)}, u32[]{:S(2)}) async-start(f32[8,8,128]{2,1,0:T(8,128)} %bitcast.54), calls=%async_computation.1 | async-start | bytes 65536 | tf_op jit(solution)/shard_map/all_to_all | solution.py:174
  45.1 35.4 %slice-start.2 = ((bf16[8,4,2,64,256]{4,3,2,1,0:T(8,128)(2,1)}), bf16[1,4,2,64,256]{4,3,2,1,0:T(8,128)(2,1)S(1)}, s32[]{:S(2)}) async-start(bf16[8,4,2,64,256]{4,3,2,1,0:T(8,128)(2,1)} %param.7), calls=%async_computation.8 | async-start | bytes 524288 | tf_op jit(solution)/shard_map/slice | solution.py:146
  45.2 15.9 %collective-permute-start.2 = (bf16[2,4,64,128]{3,2,1,0:T(8,128)(2,1)S(1)}, bf16[2,4,64,128]{3,2,1,0:T(8,128)(2,1)S(1)}, u32[]{:S(2)}, u32[]{:S(2)}) collective-permute-start(bf16[2,4,64,128]{3,2,1,0:T(8,128)(2,1)S(1)} %pad_maximum_fusion.5), channel_id=1, source_target_pairs={{0,3},{1,2},{2,1},{3,0},{4,5},{5,4},{6,7},{7,6},{8,11},{9,10},{10,... | collective-permute-start | bytes 393224 | tf_op jit(solution)/shard_map/ppermute | solution.py:123
  57.1 43.9 %slice-start.3 = ((bf16[8,4,2,64,256]{4,3,2,1,0:T(8,128)(2,1)}), bf16[1,4,2,64,256]{4,3,2,1,0:T(8,128)(2,1)S(1)}, s32[]{:S(2)}) async-start(bf16[8,4,2,64,256]{4,3,2,1,0:T(8,128)(2,1)} %param.7), calls=%async_computation.9 | async-start | bytes 524288 | tf_op jit(solution)/shard_map/slice | solution.py:146
  57.8 14.7 %all-to-all-start.2 = ((bf16[8,16,256]{2,1,0:T(8,128)(2,1)}), bf16[8,16,256]{2,1,0:T(8,128)(2,1)S(1)}, u32[]{:S(2)}, u32[]{:S(2)}) async-start(bf16[8,16,256]{2,1,0:T(8,128)(2,1)} %broadcast_in_dim.38), calls=%async_computation.2 | async-start | bytes 131072 | tf_op jit(solution)/shard_map/all_to_all | solution.py:171
  73.0 7.2 %collective-permute-start.3 = (bf16[8,128]{1,0:T(8,128)(2,1)S(1)}, bf16[8,128]{1,0:T(8,128)(2,1)S(1)}, u32[]{:S(2)}, u32[]{:S(2)}) collective-permute-start(bf16[8,128]{1,0:T(8,128)(2,1)S(1)} %fusion.156), channel_id=1, source_target_pairs={{0,16},{4,20},{8,24},{12,28},{16,0},{20,4},{24,8},{28,12},{32,48},... | collective-permute-start | bytes 6152 | tf_op jit(solution)/shard_map/ppermute | solution.py:140
  77.7 14.0 %collective-permute-start.5 = (bf16[2,4,64,128]{3,2,1,0:T(8,128)(2,1)S(1)}, bf16[2,4,64,128]{3,2,1,0:T(8,128)(2,1)S(1)}, u32[]{:S(2)}, u32[]{:S(2)}) collective-permute-start(bf16[2,4,64,128]{3,2,1,0:T(8,128)(2,1)S(1)} %pad_maximum_fusion.7), channel_id=1, source_target_pairs={{0,3},{1,2},{2,1},{3,0},{4,5},{5,4},{6,7},{7,6},{8,11},{9,10},{10,... | collective-permute-start | bytes 393224 | tf_op jit(solution)/shard_map/ppermute | solution.py:123
  80.9 51.6 %slice-start.4 = ((bf16[8,4,2,64,256]{4,3,2,1,0:T(8,128)(2,1)}), bf16[1,4,2,64,256]{4,3,2,1,0:T(8,128)(2,1)S(1)}, s32[]{:S(2)}) async-start(bf16[8,4,2,64,256]{4,3,2,1,0:T(8,128)(2,1)} %param.7), calls=%async_computation.10 | async-start | bytes 524288 | tf_op jit(solution)/shard_map/slice | solution.py:146
  81.5 19.2 %all-to-all-start.3 = ((f32[8,8,128]{2,1,0:T(8,128)}), f32[8,8,128]{2,1,0:T(8,128)S(1)}, u32[]{:S(2)}, u32[]{:S(2)}) async-start(f32[8,8,128]{2,1,0:T(8,128)} %bitcast.76), calls=%async_computation.3 | async-start | bytes 65536 | tf_op jit(solution)/shard_map/all_to_all | solution.py:174
  91.7 56.5 %copy-start.2 = (s32[4,256]{1,0:T(4,128)S(1)}, s32[4,256]{1,0:T(4,128)}, u32[]{:S(2)}) copy-start(s32[4,256]{1,0:T(4,128)} %param.5) | copy-start | bytes 12292
  101.9 29.8 %all-to-all-start.4 = ((bf16[8,16,256]{2,1,0:T(8,128)(2,1)}), bf16[8,16,256]{2,1,0:T(8,128)(2,1)S(1)}, u32[]{:S(2)}, u32[]{:S(2)}) async-start(bf16[8,16,256]{2,1,0:T(8,128)(2,1)} %broadcast_in_dim.77), calls=%async_computation.4 | async-start | bytes 131072 | tf_op jit(solution)/shard_map/all_to_all | solution.py:171

commit v6 on v5

--- a/solution.py
+++ b/solution.py
@@ -54,13 +54,11 @@
 
 def put_back(state, order):
     high = state.astype(BF16)
-    rest = state - high.astype(F32)
-    middle = rest.astype(BF16)
-    low = (rest - middle.astype(F32)).astype(BF16)
-    pieces = jnp.concatenate([high, middle, low], axis=0).reshape(3, 4, 4, 256)
+    rest = (state - high.astype(F32)).astype(BF16)
+    pieces = jnp.concatenate([high, rest], axis=0).reshape(2, 4, 4, 256)
     pick = (jnp.arange(256)[None, :, None] == order[:, None, :]).astype(BF16)
     put = jnp.einsum("pblj,bij->pbli", pieces, pick, preferred_element_type=F32)
-    return put[0] + put[1] + put[2]
+    return put[0] + put[1]
 
 
 def pair_groups(leaves, ranks, bit):

time: 150 us -> 150 us (level)
  no operation moved by 1% of the time
where the time goes in v6:
time: 150 us; the launch traced here: 149 us
  starting transfers between devices  75.6 us (50%)
  waiting for transfers between devices  44.5 us (30%)
  blocking collectives  15.4 us (10%)
  local copies, waits for them, and re-layouts  6.99 us (5%)
  other arithmetic  4.08 us (3%)
  matrix products  1.98 us (1%)
    ppermute x4, starting transfers between devices, moved_on(): return lax.ppermute(jnp.stack(pieces), ('leaf', 'rank'), route)  29.7 us
    all_to_all x2, waiting for transfers between devices, local(): lax.all_to_all(sent, ('leaf', 'rank'), 0, 0, axis_index_groups=groups, ti...  23.6 us
    all_to_all x2, starting transfers between devices, local(): lax.all_to_all(sent, ('leaf', 'rank'), 0, 0, axis_index_groups=groups, ti...  20.8 us
    all_to_all x3, waiting for transfers between devices, local(): lax.all_to_all(chunks(part, 2), ('leaf', 'rank'), 0, 0, axis_index_groups...  17.6 us
    all_to_all x1, blocking collectives, local(): whole = lax.all_to_all(sent, 'rank', 0, 0, tiled=True).astype(F32).sum(0)  15.4 us
    all_to_all x3, starting transfers between devices, local(): lax.all_to_all(chunks(part, 2), ('leaf', 'rank'), 0, 0, axis_index_groups...  14.9 us
    ppermute x1, starting transfers between devices, local(): lax.ppermute(own, 'leaf', [(at, at ^ 1 << leaf_bits - 1) for at in range(...  5.64 us
    ppermute x1, starting transfers between devices, local(): lax.ppermute(own.astype(BF16), 'leaf', [(at, at ^ 1 << bit) for at in ran...  4.65 us
  transfers between devices with their start and end apart: 11, of which 6 were waited for; matrix products, arithmetic and copies ran while one was open for 6% of the time, Pallas kernels for 0%

profile of v6, /device:TPU:1, one launch (start us, length us, event | category | flops | bytes accessed | tf_op | source)
XLA Modules:
  0.0 149.1 jit_solution(7032898869016210756)
XLA Ops:
  0.0 0.8 constant_dynamic-slice_fusion
  0.8 0.2 convolution_bitcast_fusion.1
  1.1 5.6 %collective-permute-start = (f32[8,128]{1,0:T(8,128)S(1)}, f32[8,128]{1,0:T(8,128)S(1)}, u32[]{:S(2)}, u32[]{:S(2)}) collective-permute-start(f32[8,128]{1,0:T(8,128)S(1)} %pad_maximum_fusion.12), channel_id=1, source_target_pairs={{0,256},{4,260},{8,264},{12,268},{16,272},{20,276},{24,280},{28,28... | collective-permute-start | bytes 12296 | tf_op jit(solution)/shard_map/ppermute | solution.py:111
  6.8 1.2 slice_bitcast_fusion
  8.0 0.3 slice_bitcast_fusion.15
  8.3 0.1 maximum_bitcast_fusion.4
  8.4 0.1 maximum_bitcast_fusion.5
  8.5 0.1 maximum_bitcast_fusion.6
  8.6 0.1 maximum_bitcast_fusion.7
  8.7 0.1 maximum_bitcast_fusion
  8.8 0.1 maximum_bitcast_fusion.1
  8.9 0.1 maximum_bitcast_fusion.2
  9.0 0.1 maximum_bitcast_fusion.3
  9.2 0.1 broadcast_compare_fusion
  9.4 0.1 copy.39
  9.5 0.1 broadcast_in_dim.32
  9.6 0.1 reshape.134
  9.7 12.6 %collective-permute-start.4 = (bf16[2,4,64,128]{3,2,1,0:T(8,128)(2,1)S(1)}, bf16[2,4,64,128]{3,2,1,0:T(8,128)(2,1)S(1)}, u32[]{:S(2)}, u32[]{:S(2)}) collective-permute-start(bf16[2,4,64,128]{3,2,1,0:T(8,128)(2,1)S(1)} %pad_maximum_fusion.6), channel_id=1, source_target_pairs={{0,1},{1,0},{2,3},{3,2},{4,7},{5,6},{6,5},{7,4},{8,9},{9,8},{10,11... | collective-permute-start | bytes 393224 | tf_op jit(solution)/shard_map/ppermute | solution.py:121
  22.5 0.1 fusion.128
  22.5 0.2 fusion.29
  22.8 0.1 fusion.130
  22.9 0.6 broadcast_in_dim.34
  23.5 4.7 %all-to-all-start = ((f32[8,8,128]{2,1,0:T(8,128)}), f32[8,8,128]{2,1,0:T(8,128)S(1)}, u32[]{:S(2)}, u32[]{:S(2)}) async-start(f32[8,8,128]{2,1,0:T(8,128)} %bitcast.47), calls=%async_computation | async-start | bytes 65536 | tf_op jit(solution)/shard_map/all_to_all | solution.py:172
  28.2 7.3 %collective-permute-start.1 = (bf16[2,4,64,128]{3,2,1,0:T(8,128)(2,1)S(1)}, bf16[2,4,64,128]{3,2,1,0:T(8,128)(2,1)S(1)}, u32[]{:S(2)}, u32[]{:S(2)}) collective-permute-start(bf16[2,4,64,128]{3,2,1,0:T(8,128)(2,1)S(1)} %pad_maximum_fusion.4), channel_id=1, source_target_pairs={{0,1},{1,0},{2,3},{3,2},{4,7},{5,6},{6,5},{7,4},{8,9},{9,8},{10,11... | collective-permute-start | bytes 393224 | tf_op jit(solution)/shard_map/ppermute | solution.py:121
  35.5 0.2 convert_reduce_fusion.5
  35.8 0.1 broadcast_in_dim_reshape.6
  35.9 0.1 broadcast_in_dim_reshape.7
  36.0 4.5 %all-to-all-done = f32[8,8,128]{2,1,0:T(8,128)S(1)} async-done(((f32[8,8,128]{2,1,0:T(8,128)}), f32[8,8,128]{2,1,0:T(8,128)S(1)}, u32[]{:S(2)}, u32[]{:S(2)}) %all-to-all-start) | async-done | bytes 32800 | tf_op jit(solution)/shard_map/all_to_all | solution.py:172
  40.8 0.2 fusion.44
  41.1 0.1 fusion.136
  41.2 0.6 broadcast_in_dim.37
  41.8 3.3 %all-to-all-start.1 = ((f32[8,8,128]{2,1,0:T(8,128)}), f32[8,8,128]{2,1,0:T(8,128)S(1)}, u32[]{:S(2)}, u32[]{:S(2)}) async-start(f32[8,8,128]{2,1,0:T(8,128)} %bitcast.54), calls=%async_computation.1 | async-start | bytes 65536 | tf_op jit(solution)/shard_map/all_to_all | solution.py:172
  45.2 7.3 %collective-permute-start.2 = (bf16[2,4,64,128]{3,2,1,0:T(8,128)(2,1)S(1)}, bf16[2,4,64,128]{3,2,1,0:T(8,128)(2,1)S(1)}, u32[]{:S(2)}, u32[]{:S(2)}) collective-permute-start(bf16[2,4,64,128]{3,2,1,0:T(8,128)(2,1)S(1)} %pad_maximum_fusion.5), channel_id=1, source_target_pairs={{0,3},{1,2},{2,1},{3,0},{4,5},{5,4},{6,7},{7,6},{8,11},{9,10},{10,... | collective-permute-start | bytes 393224 | tf_op jit(solution)/shard_map/ppermute | solution.py:121
  52.5 4.1 %all-to-all-done.1 = f32[8,8,128]{2,1,0:T(8,128)S(1)} async-done(((f32[8,8,128]{2,1,0:T(8,128)}), f32[8,8,128]{2,1,0:T(8,128)S(1)}, u32[]{:S(2)}, u32[]{:S(2)}) %all-to-all-start.1) | async-done | bytes 32800 | tf_op jit(solution)/shard_map/all_to_all | solution.py:172
  56.9 0.2 fusion.59
  57.1 0.6 broadcast_in_dim.38
  57.8 3.3 %all-to-all-start.2 = ((bf16[8,16,256]{2,1,0:T(8,128)(2,1)}), bf16[8,16,256]{2,1,0:T(8,128)(2,1)S(1)}, u32[]{:S(2)}, u32[]{:S(2)}) async-start(bf16[8,16,256]{2,1,0:T(8,128)(2,1)} %broadcast_in_dim.38), calls=%async_computation.2 | async-start | bytes 131072 | tf_op jit(solution)/shard_map/all_to_all | solution.py:169
  61.2 11.3 %all-to-all-done.2 = bf16[8,16,256]{2,1,0:T(8,128)(2,1)S(1)} async-done(((bf16[8,16,256]{2,1,0:T(8,128)(2,1)}), bf16[8,16,256]{2,1,0:T(8,128)(2,1)S(1)}, u32[]{:S(2)}, u32[]{:S(2)}) %all-to-all-start.2) | async-done | bytes 65568 | tf_op jit(solution)/shard_map/all_to_all | solution.py:169
  72.6 0.1 fusion.26
  72.7 0.2 fusion.4
  72.9 0.1 slice_add_fusion.2
  73.0 4.7 %collective-permute-start.3 = (bf16[8,128]{1,0:T(8,128)(2,1)S(1)}, bf16[8,128]{1,0:T(8,128)(2,1)S(1)}, u32[]{:S(2)}, u32[]{:S(2)}) collective-permute-start(bf16[8,128]{1,0:T(8,128)(2,1)S(1)} %fusion.155), channel_id=1, source_target_pairs={{0,16},{4,20},{8,24},{12,28},{16,0},{20,4},{24,8},{28,12},{32,48},... | collective-permute-start | bytes 6152 | tf_op jit(solution)/shard_map/ppermute | solution.py:138
  77.7 2.5 %collective-permute-start.5 = (bf16[2,4,64,128]{3,2,1,0:T(8,128)(2,1)S(1)}, bf16[2,4,64,128]{3,2,1,0:T(8,128)(2,1)S(1)}, u32[]{:S(2)}, u32[]{:S(2)}) collective-permute-start(bf16[2,4,64,128]{3,2,1,0:T(8,128)(2,1)S(1)} %pad_maximum_fusion.7), channel_id=1, source_target_pairs={{0,3},{1,2},{2,1},{3,0},{4,5},{5,4},{6,7},{7,6},{8,11},{9,10},{10,... | collective-permute-start | bytes 393224 | tf_op jit(solution)/shard_map/ppermute | solution.py:121
  80.4 0.1 fusion.142
  80.5 0.2 fusion.74
  80.8 0.1 fusion.144
  80.9 0.6 broadcast_in_dim.76
  81.5 6.9 %all-to-all-start.3 = ((f32[8,8,128]{2,1,0:T(8,128)}), f32[8,8,128]{2,1,0:T(8,128)S(1)}, u32[]{:S(2)}, u32[]{:S(2)}) async-start(f32[8,8,128]{2,1,0:T(8,128)} %bitcast.76), calls=%async_computation.3 | async-start | bytes 65536 | tf_op jit(solution)/shard_map/all_to_all | solution.py:172
  88.4 3.3 %collective-permute-done.5 = bf16[2,4,64,128]{3,2,1,0:T(8,128)(2,1)S(1)} collective-permute-done((bf16[2,4,64,128]{3,2,1,0:T(8,128)(2,1)S(1)}, bf16[2,4,64,128]{3,2,1,0:T(8,128)(2,1)S(1)}, u32[]{:S(2)}, u32[]{:S(2)}) %collective-permute-start.5) | collective-permute-done | bytes 131104 | tf_op jit(solution)/shard_map/ppermute | solution.py:121
  91.7 9.0 %all-to-all-done.3 = f32[8,8,128]{2,1,0:T(8,128)S(1)} async-done(((f32[8,8,128]{2,1,0:T(8,128)}), f32[8,8,128]{2,1,0:T(8,128)S(1)}, u32[]{:S(2)}, u32[]{:S(2)}) %all-to-all-start.3) | async-done | bytes 32800 | tf_op jit(solution)/shard_map/all_to_all | solution.py:172
  101.0 0.2 fusion.89
  101.2 0.6 broadcast_in_dim.77
  101.9 17.4 %all-to-all-start.4 = ((bf16[8,16,256]{2,1,0:T(8,128)(2,1)}), bf16[8,16,256]{2,1,0:T(8,128)(2,1)S(1)}, u32[]{:S(2)}, u32[]{:S(2)}) async-start(bf16[8,16,256]{2,1,0:T(8,128)(2,1)} %broadcast_in_dim.77), calls=%async_computation.4 | async-start | bytes 131072 | tf_op jit(solution)/shard_map/all_to_all | solution.py:169
  119.4 12.3 %all-to-all-done.4 = bf16[8,16,256]{2,1,0:T(8,128)(2,1)S(1)} async-done(((bf16[8,16,256]{2,1,0:T(8,128)(2,1)}), bf16[8,16,256]{2,1,0:T(8,128)(2,1)S(1)}, u32[]{:S(2)}, u32[]{:S(2)}) %all-to-all-start.4) | async-done | bytes 65568 | tf_op jit(solution)/shard_map/all_to_all | solution.py:169
  131.7 0.1 multiply_convert_fusion
  131.8 0.1 fusion.23
  131.9 0.2 fusion.11
  132.1 0.1 slice_add_fusion.1
  132.2 0.1 bitcast_multiply_fusion
  132.4 0.1 fusion.150
  132.5 0.2 fusion.104
  132.7 15.4 %all_to_all.30 = bf16[4,16,256]{2,1,0:T(8,128)(2,1)S(1)} all-to-all(bf16[4,16,256]{2,1,0:T(8,128)(2,1)S(1)} %broadcast_in_dim.78), channel_id=1, replica_groups=mesh['leaf'=128,'rank'=4] {'rank'}, dimensions={0} | all-to-all | bytes 65536 | tf_op jit(solution)/shard_map/all_to_all | solution.py:179
  148.2 0.3 convolution_bitcast_fusion
  148.4 0.6 fusion.28
  (93 shorter events, 2.6 us)
Async XLA Ops:
  0.0 0.8 copy-start
  1.1 8.6 %collective-permute-start = (f32[8,128]{1,0:T(8,128)S(1)}, f32[8,128]{1,0:T(8,128)S(1)}, u32[]{:S(2)}, u32[]{:S(2)}) collective-permute-start(f32[8,128]{1,0:T(8,128)S(1)} %pad_maximum_fusion.12), channel_id=1, source_target_pairs={{0,256},{4,260},{8,264},{12,268},{16,272},{20,276},{24,280},{28,28... | collective-permute-start | bytes 12296 | tf_op jit(solution)/shard_map/ppermute | solution.py:111
  8.3 1.1 copy-start.1
  9.1 31.8 %slice-start = ((bf16[8,4,2,64,256]{4,3,2,1,0:T(8,128)(2,1)}), bf16[1,4,2,64,256]{4,3,2,1,0:T(8,128)(2,1)S(1)}, s32[]{:S(2)}) async-start(bf16[8,4,2,64,256]{4,3,2,1,0:T(8,128)(2,1)} %param.7), calls=%async_computation.6 | async-start | bytes 524288 | tf_op jit(solution)/shard_map/slice | solution.py:144
  9.7 47.3 %slice-start.1 = ((bf16[8,4,2,64,256]{4,3,2,1,0:T(8,128)(2,1)}), bf16[1,4,2,64,256]{4,3,2,1,0:T(8,128)(2,1)S(1)}, s32[]{:S(2)}) async-start(bf16[8,4,2,64,256]{4,3,2,1,0:T(8,128)(2,1)} %param.7), calls=%async_computation.7 | async-start | bytes 524288 | tf_op jit(solution)/shard_map/slice | solution.py:144
  9.7 42.8 %collective-permute-start.4 = (bf16[2,4,64,128]{3,2,1,0:T(8,128)(2,1)S(1)}, bf16[2,4,64,128]{3,2,1,0:T(8,128)(2,1)S(1)}, u32[]{:S(2)}, u32[]{:S(2)}) collective-permute-start(bf16[2,4,64,128]{3,2,1,0:T(8,128)(2,1)S(1)} %pad_maximum_fusion.6), channel_id=1, source_target_pairs={{0,1},{1,0},{2,3},{3,2},{4,7},{5,6},{6,5},{7,4},{8,9},{9,8},{10,11... | collective-permute-start | bytes 393224 | tf_op jit(solution)/shard_map/ppermute | solution.py:121
  23.5 17.0 %all-to-all-start = ((f32[8,8,128]{2,1,0:T(8,128)}), f32[8,8,128]{2,1,0:T(8,128)S(1)}, u32[]{:S(2)}, u32[]{:S(2)}) async-start(f32[8,8,128]{2,1,0:T(8,128)} %bitcast.47), calls=%async_computation | async-start | bytes 65536 | tf_op jit(solution)/shard_map/all_to_all | solution.py:172
  28.2 17.0 %collective-permute-start.1 = (bf16[2,4,64,128]{3,2,1,0:T(8,128)(2,1)S(1)}, bf16[2,4,64,128]{3,2,1,0:T(8,128)(2,1)S(1)}, u32[]{:S(2)}, u32[]{:S(2)}) collective-permute-start(bf16[2,4,64,128]{3,2,1,0:T(8,128)(2,1)S(1)} %pad_maximum_fusion.4), channel_id=1, source_target_pairs={{0,1},{1,0},{2,3},{3,2},{4,7},{5,6},{6,5},{7,4},{8,9},{9,8},{10,11... | collective-permute-start | bytes 393224 | tf_op jit(solution)/shard_map/ppermute | solution.py:121
  41.8 14.8 %all-to-all-start.1 = ((f32[8,8,128]{2,1,0:T(8,128)}), f32[8,8,128]{2,1,0:T(8,128)S(1)}, u32[]{:S(2)}, u32[]{:S(2)}) async-start(f32[8,8,128]{2,1,0:T(8,128)} %bitcast.54), calls=%async_computation.1 | async-start | bytes 65536 | tf_op jit(solution)/shard_map/all_to_all | solution.py:172
  45.1 35.4 %slice-start.2 = ((bf16[8,4,2,64,256]{4,3,2,1,0:T(8,128)(2,1)}), bf16[1,4,2,64,256]{4,3,2,1,0:T(8,128)(2,1)S(1)}, s32[]{:S(2)}) async-start(bf16[8,4,2,64,256]{4,3,2,1,0:T(8,128)(2,1)} %param.7), calls=%async_computation.8 | async-start | bytes 524288 | tf_op jit(solution)/shard_map/slice | solution.py:144
  45.2 15.9 %collective-permute-start.2 = (bf16[2,4,64,128]{3,2,1,0:T(8,128)(2,1)S(1)}, bf16[2,4,64,128]{3,2,1,0:T(8,128)(2,1)S(1)}, u32[]{:S(2)}, u32[]{:S(2)}) collective-permute-start(bf16[2,4,64,128]{3,2,1,0:T(8,128)(2,1)S(1)} %pad_maximum_fusion.5), channel_id=1, source_target_pairs={{0,3},{1,2},{2,1},{3,0},{4,5},{5,4},{6,7},{7,6},{8,11},{9,10},{10,... | collective-permute-start | bytes 393224 | tf_op jit(solution)/shard_map/ppermute | solution.py:121
  57.1 43.9 %slice-start.3 = ((bf16[8,4,2,64,256]{4,3,2,1,0:T(8,128)(2,1)}), bf16[1,4,2,64,256]{4,3,2,1,0:T(8,128)(2,1)S(1)}, s32[]{:S(2)}) async-start(bf16[8,4,2,64,256]{4,3,2,1,0:T(8,128)(2,1)} %param.7), calls=%async_computation.9 | async-start | bytes 524288 | tf_op jit(solution)/shard_map/slice | solution.py:144
  57.8 14.7 %all-to-all-start.2 = ((bf16[8,16,256]{2,1,0:T(8,128)(2,1)}), bf16[8,16,256]{2,1,0:T(8,128)(2,1)S(1)}, u32[]{:S(2)}, u32[]{:S(2)}) async-start(bf16[8,16,256]{2,1,0:T(8,128)(2,1)} %broadcast_in_dim.38), calls=%async_computation.2 | async-start | bytes 131072 | tf_op jit(solution)/shard_map/all_to_all | solution.py:169
  73.0 7.2 %collective-permute-start.3 = (bf16[8,128]{1,0:T(8,128)(2,1)S(1)}, bf16[8,128]{1,0:T(8,128)(2,1)S(1)}, u32[]{:S(2)}, u32[]{:S(2)}) collective-permute-start(bf16[8,128]{1,0:T(8,128)(2,1)S(1)} %fusion.155), channel_id=1, source_target_pairs={{0,16},{4,20},{8,24},{12,28},{16,0},{20,4},{24,8},{28,12},{32,48},... | collective-permute-start | bytes 6152 | tf_op jit(solution)/shard_map/ppermute | solution.py:138
  77.7 14.0 %collective-permute-start.5 = (bf16[2,4,64,128]{3,2,1,0:T(8,128)(2,1)S(1)}, bf16[2,4,64,128]{3,2,1,0:T(8,128)(2,1)S(1)}, u32[]{:S(2)}, u32[]{:S(2)}) collective-permute-start(bf16[2,4,64,128]{3,2,1,0:T(8,128)(2,1)S(1)} %pad_maximum_fusion.7), channel_id=1, source_target_pairs={{0,3},{1,2},{2,1},{3,0},{4,5},{5,4},{6,7},{7,6},{8,11},{9,10},{10,... | collective-permute-start | bytes 393224 | tf_op jit(solution)/shard_map/ppermute | solution.py:121
  80.9 51.6 %slice-start.4 = ((bf16[8,4,2,64,256]{4,3,2,1,0:T(8,128)(2,1)}), bf16[1,4,2,64,256]{4,3,2,1,0:T(8,128)(2,1)S(1)}, s32[]{:S(2)}) async-start(bf16[8,4,2,64,256]{4,3,2,1,0:T(8,128)(2,1)} %param.7), calls=%async_computation.10 | async-start | bytes 524288 | tf_op jit(solution)/shard_map/slice | solution.py:144
  81.5 19.2 %all-to-all-start.3 = ((f32[8,8,128]{2,1,0:T(8,128)}), f32[8,8,128]{2,1,0:T(8,128)S(1)}, u32[]{:S(2)}, u32[]{:S(2)}) async-start(f32[8,8,128]{2,1,0:T(8,128)} %bitcast.76), calls=%async_computation.3 | async-start | bytes 65536 | tf_op jit(solution)/shard_map/all_to_all | solution.py:172
  91.7 56.5 %copy-start.2 = (s32[4,256]{1,0:T(4,128)S(1)}, s32[4,256]{1,0:T(4,128)}, u32[]{:S(2)}) copy-start(s32[4,256]{1,0:T(4,128)} %param.5) | copy-start | bytes 12292
  101.9 29.8 %all-to-all-start.4 = ((bf16[8,16,256]{2,1,0:T(8,128)(2,1)}), bf16[8,16,256]{2,1,0:T(8,128)(2,1)S(1)}, u32[]{:S(2)}, u32[]{:S(2)}) async-start(bf16[8,16,256]{2,1,0:T(8,128)(2,1)} %broadcast_in_dim.77), calls=%async_computation.4 | async-start | bytes 131072 | tf_op jit(solution)/shard_map/all_to_all | solution.py:169
